TPU v7x, 128 devices: a whole 4x4x4 slice. The times are simulated.
128 devices in a mesh: gx: 8 (over x, core), gy: 16 (over y, z).
Axes of the slice: x: 4, y: 4, z: 4, core: 2. Of those that a mesh axis runs over, the one named last changes fastest.
Arguments:
- features: bfloat16 [8, 16, 2, 96, 4096], P('gx', 'gy'), may hold values from -6 to 6
- grad_out: bfloat16 [8, 16, 2, 96, 4096], P('gx', 'gy'), may hold values from -6 to 6
- weight: bfloat16 [96, 2592], replicated, may hold values from -0.125 to 0.125
- active: int32 [8, 16, 2], P('gx', 'gy'), may hold values from 0 to 1, as said below
Outputs:
- out: bfloat16 [8, 16, 2, 96, 4096], P('gx', 'gy')
- grad_in: bfloat16 [8, 16, 2, 96, 4096], P('gx', 'gy')
- grad_weight: float32 [248832], P(('gx', 'gy'))
Inputs may be any that keep to these rules, and one draw needn't show every extreme that they name: The two columns with the same gx index and gy indices 2m and 2m + 1 hold exactly 2 active bricks together, so a column holds 0 to 2 of them; some column holds 2 in every draw.
All inputs are finite; a program needn't handle non-finite values.
Results may differ from a plain program's by a relative error of at most 0.001.
Values may be sent and summed in bfloat16 or wider, within the bound.
No kernel may reach another device: no remote copies, remote signals or barrier semaphores. Data moves between devices by JAX's collectives and lax.ppermute only.
A program may use at most 128 MiB of HBM per device.

v0:
```python
import math

import jax
import jax.numpy as jnp
from jax import lax
from jax.sharding import PartitionSpec as P

EDGE = 16


def extended(block, sides, width):
    for axis, dim in sides:
        count = lax.axis_size(axis)
        forward = [(i, i + 1) for i in range(count - 1)]
        backward = [(target, source) for source, target in forward]
        low = lax.ppermute(
            lax.slice_in_dim(block, block.shape[dim] - width, None, axis=dim), axis, forward
        )
        high = lax.ppermute(lax.slice_in_dim(block, 0, width, axis=dim), axis, backward)
        block = jnp.concatenate([low, block, high], axis=dim)
    return block


def body(features, grad_out, weight, active):
    levels = features.shape[2]
    channels = features.shape[3]
    cube_side = EDGE
    padded_side = cube_side + 2
    plane_cells = padded_side * padded_side
    first_cell = plane_cells + padded_side + 1
    range_len = (cube_side - 1) * first_cell + 1
    shift_list = [
        offset_x * plane_cells + offset_y * padded_side + offset_z
        for offset_x in (-1, 0, 1)
        for offset_y in (-1, 0, 1)
        for offset_z in (-1, 0, 1)
    ]
    cell_ids = jnp.arange(range_len)
    inside = (cell_ids // padded_side % padded_side < cube_side) & (
        cell_ids % padded_side < cube_side
    )
    inside_flags = inside.astype(jnp.bfloat16)[None, :]
    side_ids = jnp.arange(padded_side)
    side_out = (side_ids == 0) | (side_ids == padded_side - 1)
    edge_keep = jnp.logical_not(side_out[:, None] & side_out[None, :]).astype(jnp.bfloat16)[
        :, :, None
    ]
    live_mask = active[0, 0]
    live_flags = live_mask.astype(jnp.bfloat16)[None, :, None, None]
    stacked = jnp.stack([features[0, 0], grad_out[0, 0]]) * live_flags
    bricks = stacked.reshape(2, levels, channels, cube_side, cube_side, cube_side)
    rimmed = extended(bricks, (("gx", 3), ("gy", 4)), 1)
    rimmed = rimmed * edge_keep
    zero_plane = jnp.zeros((2, 1, channels, cube_side, cube_side), jnp.bfloat16)
    below_rim = jnp.concatenate([zero_plane, bricks[:, :-1, :, :, :, cube_side - 1]], axis=1)
    above_rim = jnp.concatenate([bricks[:, 1:, :, :, :, 0], zero_plane], axis=1)
    rim_pad = ((0, 0), (0, 0), (0, 0), (1, 1), (1, 1))
    padded = jnp.concatenate(
        [jnp.pad(below_rim, rim_pad)[..., None], rimmed, jnp.pad(above_rim, rim_pad)[..., None]],
        axis=5,
    )
    flattened = padded.reshape(2, levels, channels, padded_side**3)
    back_weight = (
        weight.reshape(channels, 27, channels).transpose(2, 1, 0).reshape(channels, 27 * channels)
    )

    def unroll(values):
        grown = jnp.pad(values, ((0, 0), (0, cube_side * plane_cells - range_len)))
        grown = grown.reshape(values.shape[0], cube_side, padded_side, padded_side)
        return grown[:, :, :cube_side, :cube_side].reshape(values.shape[0], cube_side**3)

    def brick_work(brick_pair):
        field_pad = brick_pair[0]
        grad_pad = brick_pair[1]
        grad_cells = grad_pad[:, first_cell : first_cell + range_len] * inside_flags
        forward_res = jnp.zeros((channels, range_len), jnp.float32)
        backward_res = jnp.zeros((channels, range_len), jnp.float32)
        weight_blocks = []
        for offset_at, shift_by in enumerate(shift_list):
            field_slice = lax.slice_in_dim(
                field_pad, first_cell + shift_by, first_cell + shift_by + range_len, axis=1
            )
            grad_slice = lax.slice_in_dim(
                grad_pad, first_cell - shift_by, first_cell - shift_by + range_len, axis=1
            )
            low = offset_at * channels
            forward_res = forward_res + jnp.dot(
                weight[:, low : low + channels], field_slice, preferred_element_type=jnp.float32
            )
            backward_res = backward_res + jnp.dot(
                back_weight[:, low : low + channels], grad_slice, preferred_element_type=jnp.float32
            )
            weight_blocks.append(
                lax.dot_general(
                    grad_cells,
                    field_slice,
                    (((1,), (1,)), ((), ())),
                    preferred_element_type=jnp.float32,
                )
            )
        grad_part = jnp.concatenate(weight_blocks, axis=1)
        pair_out = jnp.stack([unroll(forward_res), unroll(backward_res)]).astype(jnp.bfloat16)
        return (pair_out, grad_part)

    def skipped(brick_pair):
        return (
            jnp.zeros((2, channels, cube_side**3), jnp.bfloat16),
            jnp.zeros((channels, 27 * channels), jnp.float32),
        )

    results = []
    grad_local = jnp.zeros((channels, 27 * channels), jnp.float32)
    for level_at in range(levels):
        pair_out, grad_part = lax.cond(
            live_mask[level_at] > 0, brick_work, skipped, flattened[:, level_at]
        )
        results.append(pair_out)
        grad_local = grad_local + grad_part
    out_pairs = jnp.stack(results, axis=1)
    summed = lax.psum_scatter(grad_local.reshape(-1), ("gx", "gy"), scatter_dimension=0, tiled=True)
    norm_scale = 1.0 / math.sqrt(lax.axis_size("gx") * lax.axis_size("gy") * levels * cube_side**3)
    return (out_pairs[0][None, None], out_pairs[1][None, None], summed * norm_scale)


def solution(mesh):
    placed = (
        P("gx", "gy", None, None, None),
        P("gx", "gy", None, None, None),
        P(),
        P("gx", "gy", None),
    )
    return jax.shard_map(
        body,
        mesh=mesh,
        in_specs=placed,
        out_specs=(
            P("gx", "gy", None, None, None),
            P("gx", "gy", None, None, None),
            P(("gx", "gy")),
        ),
        check_vma=False,
    )
```

profile of v0, /device:TPU:1, one launch (start us, length us, event | category | flops | bytes accessed | tf_op | source)
XLA Modules:
  0.0 448.8 jit_solution(2352715559401727340)
XLA Ops:
  7.2 3.0 copy.73
  10.3 3.9 copy.72
  17.5 4.5 collective-permute-start
  31.2 3.6 collective-permute-start.2
  36.1 2.6 collective-permute-done.2
  38.8 4.1 collective-permute-done.3
  42.9 4.3 maximum_multiply_fusion
  47.2 4.9 %pad_maximum_fusion.2 = bf16[2,2,96,18,18,18]{2,5,4,3,1,0:T(8,128)(2,1)S(1)} fusion(bf16[2,2,96,18,18,1]{2,5,4,3,1,0:T(2,128)(2,1)S(1)} %copy.77, bf16[2,2,96,18,18,16]{2,5,4,3,1,0:T(8,128)(2,1)S(1)} %maximum_multiply_fusion, bf16[2,2,96,18,18,1]{2,5,4,3,1,0:T(2,128)(2,1)S(1)} %copy.76), kind=kLoop, calls=%fused_computation.444 | loop fusion | flops 13436928 | bytes 8957952 | tf_op jit(solution)/shard_map/concatenate | solution.py:58
  52.2 4.5 %copy.78 = bf16[2,2,96,18,18,18]{2,1,5,4,3,0:T(2,128)(2,1)} copy(bf16[2,2,96,18,18,18]{2,5,4,3,1,0:T(8,128)(2,1)S(1)} %pad_maximum_fusion.2) | data formatting | bytes 8957952 | tf_op jit(solution)/shard_map/concatenate | solution.py:58
  56.7 118.4 %conditional.3 = (f32[96,2592]{1,0:T(8,128)}, bf16[2,1,96,4096]{3,2,1,0:T(8,128)(2,1)}) conditional(s32[]{:T(128)} %bitcast.18, () %tuple.30, (bf16[2,2,96,5832]{2,1,3,0:T(2,128)(2,1)}, bf16[1,5146]{1,0:T(2,128)(2,1)S(1)}, bf16[96,2592]{1,0:T(8,128)(2,1)S(1)}, bf16[96,2592]{0,1:T(8,128)(2,1)S(1)}) %tuple.62), branch_computations={%region_2.3_spmd, %region_3.4_spmd} | conditional | flops 7723742720 | bytes 363917504 | solution.py:114
  56.7 14.3 %copy.83 = bf16[2,2,96,5832]{3,2,1,0:T(8,128)(2,1)} copy(bf16[2,2,96,5832]{2,1,3,0:T(2,128)(2,1)} %get-tuple-element.69) | data formatting | bytes 8957952 | tf_op jit(solution)/shard_map
  90.6 2.6 pad.22.clone
  93.3 3.5 reshape.234
  119.4 2.6 pad.23.clone
  122.0 3.5 reshape.235
  128.9 3.9 copy.94
  175.1 99.4 %conditional.2 = (f32[96,2592]{1,0:T(8,128)}, bf16[2,1,96,4096]{3,2,1,0:T(8,128)(2,1)}) conditional(s32[]{:T(128)} %bitcast.8, () %tuple.28, (bf16[2,2,96,5832]{2,1,3,0:T(2,128)(2,1)}, bf16[1,5146]{1,0:T(2,128)(2,1)S(1)}, bf16[96,2592]{1,0:T(8,128)(2,1)S(1)}, bf16[96,2592]{0,1:T(8,128)(2,1)S(1)}) %tuple.63), branch_computations={%region_0.1_spmd, %region_1.2_spmd} | conditional | flops 7723742720 | bytes 363917504 | solution.py:114
  175.1 13.8 %copy.81 = bf16[2,2,96,5832]{3,2,1,0:T(8,128)(2,1)} copy(bf16[2,2,96,5832]{2,1,3,0:T(2,128)(2,1)} %get-tuple-element.65) | data formatting | bytes 8957952 | tf_op jit(solution)/shard_map
  208.5 2.6 pad.20.clone
  211.2 3.5 reshape.232
  234.7 2.6 pad.21.clone
  237.4 3.6 reshape.233
  244.3 3.9 copy.92
  283.1 157.2 %all-reduce.11.cloned.1.call-done = f32[248832]{0:T(1024)} async-done(((f32[248832]{0:T(1024)}), f32[248832]{0:T(1024)}) %all-reduce.11.cloned.1.call-update) | async-done | bytes 995344
  (224 shorter events, 177.9 us)
Async XLA Ops:
  7.2 433.2 %all-reduce.11.cloned.1.call-start = ((), (), s32[]{:S(2)}) async-start(), calls=%async_computation | async-start | bytes 1990656
  10.2 3.9 copy-start.7
  16.5 8.7 %copy-start = (bf16[2,2,96,16,16,16]{2,5,4,3,1,0:T(8,128)(2,1)}, bf16[2,2,96,16,16,16]{2,5,4,3,1,0:T(8,128)(2,1)S(1)}, u32[]{:S(2)}) copy-start(bf16[2,2,96,16,16,16]{2,5,4,3,1,0:T(8,128)(2,1)S(1)} %maximum_multiply_fusion.1) | copy-start | bytes 9437188
  17.5 10.8 %collective-permute-start = (bf16[2,2,96,1,16,16]{2,5,4,3,1,0:T(8,128)(2,1)}, bf16[2,2,96,1,16,16]{2,5,4,3,1,0:T(8,128)(2,1)S(1)}, u32[]{:S(2)}, u32[]{:S(2)}) collective-permute-start(bf16[2,2,96,1,16,16]{2,5,4,3,1,0:T(8,128)(2,1)} %get-tuple-element.83), channel_id=1, source_target_pairs={{0,16},{16,32},{32,48},{48,64},{64,80},{80,96},{96,112},{1,17},{17... | collective-permute-start | bytes 589832 | tf_op jit(solution)/shard_map/ppermute | solution.py:16
  21.9 8.0 %collective-permute-start.1 = (bf16[2,2,96,1,16,16]{2,5,4,3,1,0:T(8,128)(2,1)}, bf16[2,2,96,1,16,16]{2,5,4,3,1,0:T(8,128)(2,1)}, u32[]{:S(2)}, u32[]{:S(2)}) collective-permute-start(bf16[2,2,96,1,16,16]{2,5,4,3,1,0:T(8,128)(2,1)} %get-tuple-element.84), channel_id=1, source_target_pairs={{16,0},{32,16},{48,32},{64,48},{80,64},{96,80},{112,96},{17,1},{33... | collective-permute-start | bytes 589832 | tf_op jit(solution)/shard_map/ppermute | solution.py:19
  24.5 1.3 copy-start.2
  28.3 14.6 %copy-start.1 = (bf16[2,2,96,16,16,16]{2,5,4,3,1,0:T(8,128)(2,1)S(1)}, bf16[2,2,96,16,16,16]{2,5,4,3,1,0:T(8,128)(2,1)}, u32[]{:S(2)}) copy-start(bf16[2,2,96,16,16,16]{2,5,4,3,1,0:T(8,128)(2,1)} %copy-done) | copy-start | bytes 9437188
  31.2 7.6 %collective-permute-start.2 = (bf16[2,2,96,18,1,16]{2,5,4,3,1,0:T(8,128)(2,1)S(1)}, bf16[2,2,96,18,1,16]{2,5,4,3,1,0:T(8,128)(2,1)S(1)}, u32[]{:S(2)}, u32[]{:S(2)}) collective-permute-start(bf16[2,2,96,18,1,16]{2,5,4,3,1,0:T(8,128)(2,1)S(1)} %get-tuple-element.79), channel_id=1, source_target_pairs={{0,1},{1,2},{2,3},{3,4},{4,5},{5,6},{6,7},{7,8},{8,9},{9,10},{10,1... | collective-permute-start | bytes 663560 | tf_op jit(solution)/shard_map/ppermute | solution.py:16
  34.7 8.1 %collective-permute-start.3 = (bf16[2,2,96,18,1,16]{2,5,4,3,1,0:T(8,128)(2,1)S(1)}, bf16[2,2,96,18,1,16]{2,5,4,3,1,0:T(8,128)(2,1)S(1)}, u32[]{:S(2)}, u32[]{:S(2)}) collective-permute-start(bf16[2,2,96,18,1,16]{2,5,4,3,1,0:T(8,128)(2,1)S(1)} %get-tuple-element.80), channel_id=1, source_target_pairs={{1,0},{2,1},{3,2},{4,3},{5,4},{6,5},{7,6},{8,7},{9,8},{10,9},{11,1... | collective-permute-start | bytes 663560 | tf_op jit(solution)/shard_map/ppermute | solution.py:19
  100.4 1.3 copy-start.5
  125.6 1.5 copy-start.3
  217.6 13.8 %copy-start.6 = (bf16[96,2592]{1,0:T(8,128)(2,1)}, bf16[96,2592]{1,0:T(8,128)(2,1)S(1)}, u32[]{:S(2)}) copy-start(bf16[96,2592]{1,0:T(8,128)(2,1)S(1)} %copy.82) | copy-start | bytes 1492996 | tf_op jit(solution)/shard_map/cond
  237.4 5.0 %copy-start.4 = (bf16[96,16,16,16]{0,3,2,1:T(8,128)(2,1)S(1)}, bf16[96,16,16,16]{0,3,2,1:T(8,128)(2,1)}, u32[]{:S(2)}) copy-start(bf16[96,16,16,16]{0,3,2,1:T(8,128)(2,1)} %slice.762) | copy-start | bytes 2359300 | tf_op jit(solution)/shard_map/cond
Sparse Core Ops, SparseCore 0:
  278.1 162.2 all-reduce.10
where the time goes:
time: 457 us; the launch traced here: 449 us
  waiting for transfers between devices  166 us (36%)
  matrix products  126 us (28%)
  local copies, waits for them, and re-layouts  109 us (24%)
  other arithmetic  19.9 us (4%)
  between operations  15.7 us (3%)
  starting transfers between devices  11.3 us (2%)
    unnamed x2, waiting for transfers between devices  157 us
    dot_general x54, matrix products, brick_work(): lax.dot_general(grad_cells, field_slice, (((1,), (1,)), ((), ())), prefer...  63.3 us
    dot_general x54, matrix products, brick_work(): jnp.dot(back_weight[:, low:low + channels], grad_slice, preferred_element...  31.8 us
    dot_general x54, matrix products, brick_work(): jnp.dot(weight[:, low:low + channels], field_slice, preferred_element_typ...  30.5 us
    another operation x4, local copies, waits for them, and re-layouts  29.5 us
    reshape x4, local copies, waits for them, and re-layouts, unroll(): grown = grown.reshape(values.shape[0], cube_side, padded_side, padded_side)  14.3 us
    pad x4, local copies, waits for them, and re-layouts, unroll(): grown = jnp.pad(values, ((0, 0), (0, cube_side * plane_cells - range_len)))  10.6 us
  transfers between devices with their start and end apart: 5, of which 4 were waited for; matrix products, arithmetic and copies ran while one was open for 2% of the time, Pallas kernels for 0%

commit v1 on v0

v1 whole, which is shorter than its diff:
```python
import functools
import math

import jax
import jax.numpy as jnp
from jax import lax
from jax.experimental import pallas as pl
from jax.experimental.pallas import tpu as pltpu
from jax.sharding import PartitionSpec as P

EDGE = 16
PLANE = EDGE * EDGE
NEAR = 9
bf16 = jnp.bfloat16
f32 = jnp.float32


def lanes_of(shape):
    return lax.broadcasted_iota(jnp.int32, shape, 1)


def pick(mask, a, b):
    return jnp.where(mask, a, b)


def pack_kernel(act_ref, f_ref, g_ref, xlo_ref, xhi_ref, ylo_ref, yhi_ref):
    c = f_ref.shape[0]
    live = act_ref[0, 0, pl.program_id(0)].astype(f32).astype(bf16)
    half = lanes_of((c, 128)) // EDGE
    for arr, src in enumerate((f_ref, g_ref)):
        xlo_ref[arr] = src[:, 0:PLANE] * live
        xhi_ref[arr] = src[:, 15 * PLANE : 16 * PLANE] * live
        for h in range(2):
            low = jnp.zeros((c, 128), bf16)
            high = jnp.zeros((c, 128), bf16)
            for xs in range(8):
                x = 8 * h + xs
                a = src[:, x * PLANE : x * PLANE + 128]
                b = src[:, x * PLANE + 128 : x * PLANE + 256]
                if xs:
                    a = pltpu.roll(a, 16 * xs, 1)
                if xs != 7:
                    b = pltpu.roll(b, 16 * xs + 16, 1)
                low = pick(half == xs, a, low)
                high = pick(half == xs, b, high)
            ylo_ref[arr, :, h * 128 : h * 128 + 128] = low * live
            yhi_ref[arr, :, h * 128 : h * 128 + 128] = high * live


def pack(active, features, grads):
    levels, c, vox = features.shape
    face = jax.ShapeDtypeStruct((2, levels, c, PLANE), bf16)
    brick = pl.BlockSpec((None, c, vox), lambda k: (k, 0, 0))
    side = pl.BlockSpec((2, None, c, PLANE), lambda k: (0, k, 0, 0))
    return pl.pallas_call(
        pack_kernel,
        grid=(levels,),
        in_specs=[pl.BlockSpec(memory_space=pltpu.SMEM), brick, brick],
        out_specs=[side] * 4,
        out_shape=[face] * 4,
        name="pack_faces",
    )(active, features, grads)


def shifted_rows(y_ref, lev, ys_ref):
    c = ys_ref.shape[2]
    z = lanes_of((c, PLANE)) % EDGE
    zero = jnp.zeros((c, PLANE), bf16)
    for side in range(2):
        row = y_ref[side, lev]
        ys_ref[side, 0] = pick(z == 0, zero, pltpu.roll(row, 1, 1))
        ys_ref[side, 1] = row
        ys_ref[side, 2] = pick(z == EDGE - 1, zero, pltpu.roll(row, PLANE - 1, 1))


def fill_plane(store, plane, below, above, rows):
    c = plane.shape[0]
    lane = lanes_of((c, PLANE))
    z = lane % EDGE
    down = pltpu.roll(pick(z == EDGE - 1, pltpu.roll(below, PLANE - EDGE, 1), plane), 1, 1)
    up = pltpu.roll(pick(z == 0, pltpu.roll(above, EDGE, 1), plane), PLANE - 1, 1)
    for k, value in enumerate((down, plane, up)):
        south, north = rows(k)
        store(3 + k, value)
        store(k, pltpu.roll(pick(lane >= PLANE - EDGE, south, value), EDGE, 1))
        store(6 + k, pltpu.roll(pick(lane < EDGE, north, value), PLANE - EDGE, 1))


def build_inner(store, act_ref, src_ref, ys_ref, lev, x):
    c = src_ref.shape[1]
    other = 1 - lev
    live = act_ref[0, 0, other].astype(f32)
    start = pl.multiple_of(x * PLANE, PLANE)
    plane = src_ref[lev, :, pl.ds(start, PLANE)]
    beside = src_ref[other, :, pl.ds(start, PLANE)]
    below = beside * (live * lev.astype(f32)).astype(bf16)
    above = beside * (live * other.astype(f32)).astype(bf16)

    def rows(k):
        south = pltpu.roll(ys_ref[0, k], lax.rem(PLANE - EDGE - x * EDGE + PLANE, PLANE), 1)
        north = pltpu.roll(ys_ref[1, k], lax.rem(PLANE - x * EDGE, PLANE), 1)
        return south, north

    fill_plane(store, plane, below, above, rows)


def build_outer(store, plane):
    zero = jnp.zeros_like(plane)
    fill_plane(store, plane, zero, zero, lambda k: (zero, zero))


def conv_kernel(act_ref, src_ref, x_ref, y_ref, w_ref, out_ref, p_ref, ys_ref, acc_ref):
    lev = pl.program_id(0)
    c = src_ref.shape[1]

    @pl.when(act_ref[0, 0, lev] == 0)
    def _():
        out_ref[...] = jnp.zeros_like(out_ref)

    @pl.when(act_ref[0, 0, lev] != 0)
    def _():
        p_ref[NEAR * c :] = jnp.zeros_like(p_ref[NEAR * c :])
        shifted_rows(y_ref, lev, ys_ref)

        def store(at, value):
            p_ref[at * c : (at + 1) * c] = value

        def product():
            return jnp.dot(w_ref[...], p_ref[...], preferred_element_type=f32)

        build_outer(store, x_ref[0, lev])
        acc_ref[0] = product()[:c]
        acc_ref[1] = jnp.zeros_like(acc_ref[1])

        def step(x, _):
            build_inner(store, act_ref, src_ref, ys_ref, lev, x)
            full = product()
            done = acc_ref[1] + full[2 * c :]
            acc_ref[1] = acc_ref[0] + full[c : 2 * c]
            acc_ref[0] = full[:c]

            @pl.when(x > 0)
            def _():
                out_ref[:, pl.ds(pl.multiple_of((x - 1) * PLANE, PLANE), PLANE)] = done.astype(bf16)

            return 0

        lax.fori_loop(0, EDGE, step, 0)
        build_outer(store, x_ref[1, lev])
        full = product()
        out_ref[:, 15 * PLANE :] = (acc_ref[1] + full[2 * c :]).astype(bf16)


def conv(active, src, xface, yface, weight):
    levels, c, vox = src.shape
    depth = weight.shape[1]
    whole = pl.BlockSpec(memory_space=pltpu.VMEM)
    return pl.pallas_call(
        conv_kernel,
        grid=(levels,),
        in_specs=[pl.BlockSpec(memory_space=pltpu.SMEM)] + [whole] * 4,
        out_specs=pl.BlockSpec((None, c, vox), lambda k: (k, 0, 0)),
        out_shape=jax.ShapeDtypeStruct((levels, c, vox), bf16),
        scratch_shapes=[
            pltpu.VMEM((depth, PLANE), bf16),
            pltpu.VMEM((2, 3, c, PLANE), bf16),
            pltpu.VMEM((2, c, PLANE), f32),
        ],
        name="conv",
    )(active, src, xface, yface, weight)


def wgrad_kernel(act_ref, src_ref, grad_ref, x_ref, y_ref, out_ref, p_ref, g_ref, ys_ref):
    c = src_ref.shape[1]
    planes = EDGE + 2

    out_ref[...] = jnp.zeros_like(out_ref)
    p_ref[NEAR * c :] = jnp.zeros_like(p_ref[NEAR * c :])
    g_ref[...] = jnp.zeros_like(g_ref)

    def level(lev, _):
        @pl.when(act_ref[0, 0, lev] != 0)
        def _():
            shifted_rows(y_ref, lev, ys_ref)

            def store_at(start):
                def store(at, value):
                    p_ref[at * c : (at + 1) * c, pl.ds(start, PLANE)] = value

                return store

            for dx in range(3):
                g_ref[dx * c : (dx + 1) * c, dx * PLANE : (dx + EDGE) * PLANE] = grad_ref[lev]
            build_outer(store_at(0), x_ref[0, lev])

            def step(x, _):
                start = pl.multiple_of((x + 1) * PLANE, PLANE)
                build_inner(store_at(start), act_ref, src_ref, ys_ref, lev, x)
                return 0

            lax.fori_loop(0, EDGE, step, 0)
            build_outer(store_at((EDGE + 1) * PLANE), x_ref[1, lev])

            def gather(at, _):
                cells = pl.ds(pl.multiple_of(at * 3 * PLANE, 3 * PLANE), 3 * PLANE)
                out_ref[...] += lax.dot_general(
                    g_ref[:, cells],
                    p_ref[:, cells],
                    (((1,), (1,)), ((), ())),
                    preferred_element_type=f32,
                )
                return 0

            lax.fori_loop(0, planes // 3, gather, 0)

        return 0

    lax.fori_loop(0, 2, level, 0)


def wgrad(active, src, grads, xface, yface, depth):
    levels, c, vox = src.shape
    whole = pl.BlockSpec(memory_space=pltpu.VMEM)
    wide = (EDGE + 2) * PLANE
    return pl.pallas_call(
        wgrad_kernel,
        in_specs=[pl.BlockSpec(memory_space=pltpu.SMEM)] + [whole] * 4,
        out_specs=whole,
        out_shape=jax.ShapeDtypeStruct((3 * c, depth), f32),
        scratch_shapes=[
            pltpu.VMEM((depth, wide), bf16),
            pltpu.VMEM((3 * c, wide), bf16),
            pltpu.VMEM((2, 3, c, PLANE), bf16),
        ],
        name="wgrad",
    )(active, src, grads, xface, yface)


def neighbours(low, high, axis):
    count = lax.axis_size(axis)
    forward = [(i, i + 1) for i in range(count - 1)]
    backward = [(j, i) for i, j in forward]
    return lax.ppermute(high, axis, forward), lax.ppermute(low, axis, backward)


def body(features, grad_out, weight, active):
    levels, c, vox = features.shape[2:]
    depth = -(-NEAR * c // 128) * 128
    fields = features.reshape(levels, c, vox)
    grads = grad_out.reshape(levels, c, vox)
    xlo, xhi, ylo, yhi = pack(active, fields, grads)
    west, east = neighbours(xlo, xhi, "gx")
    south, north = neighbours(ylo, yhi, "gy")
    xfaces = jnp.stack([west, east], axis=1)
    yfaces = jnp.stack([south, north], axis=1)

    cube = weight.reshape(c, 3, NEAR, c)
    fill = ((0, 0), (0, depth - NEAR * c))
    ahead = jnp.pad(cube.transpose(1, 0, 2, 3).reshape(3 * c, NEAR * c), fill)
    back = jnp.pad(
        cube[:, ::-1, ::-1].transpose(1, 3, 2, 0).reshape(3 * c, NEAR * c), fill
    )

    gw = wgrad(active, fields, grads, xfaces[0], yfaces[0], depth)
    parts = lax.axis_size("gx") * lax.axis_size("gy")
    flat = gw[:, : NEAR * c].reshape(3, c, NEAR * c).transpose(1, 0, 2).reshape(parts, -1)
    share = flat.shape[1]
    rows = -(-share // 1024) * 8
    flat = jnp.pad(flat, ((0, 0), (0, rows * 128 - share))).reshape(parts, rows, 128)
    swapped = lax.all_to_all(flat, ("gx", "gy"), 0, 0, tiled=True)
    norm_scale = 1.0 / math.sqrt(parts * levels * vox)
    summed = swapped.sum(0).reshape(-1)[:share] * norm_scale

    out = conv(active, fields, xfaces[0], yfaces[0], ahead)
    grad_in = conv(active, grads, xfaces[1], yfaces[1], back)
    return out[None, None], grad_in[None, None], summed


def solution(mesh):
    placed = (
        P("gx", "gy", None, None, None),
        P("gx", "gy", None, None, None),
        P(),
        P("gx", "gy", None),
    )
    return jax.shard_map(
        body,
        mesh=mesh,
        in_specs=placed,
        out_specs=(
            P("gx", "gy", None, None, None),
            P("gx", "gy", None, None, None),
            P(("gx", "gy")),
        ),
        check_vma=False,
    )
```

time: 457 us -> 112 us (0.25)
  the two profiles are of different devices: /device:TPU:1 before, /device:TPU:5 now
where the time goes in v1:
time: 112 us
  Pallas kernels  73.7 us (66%)
  starting transfers between devices  21.2 us (19%)
  local copies, waits for them, and re-layouts  9.32 us (8%)
  waiting for transfers between devices  4.47 us (4%)
  other arithmetic  2.31 us (2%)
    pallas_call x2, Pallas kernels, conv(): pl.pallas_call(conv_kernel, grid=(levels,), in_specs=[pl.BlockSpec(memory...  46.4 us
    pallas_call x1, Pallas kernels, wgrad(): pl.pallas_call(wgrad_kernel, in_specs=[pl.BlockSpec(memory_space=pltpu.SM...  24.3 us
    all_to_all x1, starting transfers between devices, body(): swapped = lax.all_to_all(flat, ('gx', 'gy'), 0, 0, tiled=True)  10.8 us
    ppermute x2, starting transfers between devices, neighbours(): lax.ppermute(high, axis, forward)  7.21 us
    ppermute x2, waiting for transfers between devices, neighbours(): lax.ppermute(low, axis, backward)  4.46 us
    ppermute x2, starting transfers between devices, neighbours(): lax.ppermute(low, axis, backward)  3.21 us
    reshape x2, local copies, waits for them, and re-layouts, body(): gw[:, :NEAR * c].reshape(3, c, NEAR * c).transpose(1, 0, 2)  3.07 us
    pallas_call x1, Pallas kernels, pack(): pl.pallas_call(pack_kernel, grid=(levels,), in_specs=[pl.BlockSpec(memory...  3.06 us
  transfers between devices with their start and end apart: 5, of which 2 were waited for; matrix products, arithmetic and copies ran while one was open for 5% of the time, Pallas kernels for 41%

profile of v1, /device:TPU:5, one launch (start us, length us, event | category | flops | bytes accessed | tf_op | source)
XLA Modules:
  0.0 111.8 jit_solution(4480972722229192703)
XLA Ops:
  0.6 3.1 %pack_faces.1 = (bf16[2,2,96,256]{3,2,1,0:T(8,128)(2,1)}, bf16[2,2,96,256]{3,2,1,0:T(8,128)(2,1)}, bf16[2,2,96,256]{3,2,1,0:T(8,128)(2,1)}, bf16[2,2,96,256]{3,2,1,0:T(8,128)(2,1)}) custom-call(s32[1,1,2]{2,1,0:T(1,128)} %act_ref.7, bf16[2,96,4096]{2,1,0:T(8,128)(2,1)} %bitcast.30, bf16[2,96,4096]{2,1,0:T(8,128)(2,1)} %bitcast.33), custom_call_target="tpu_custom_call" | custom-call | tf_op jit(solution)/shard_map/pack_faces/pallas_call | solution.py:55
  3.7 3.5 %collective-permute-start.2 = (bf16[2,2,96,256]{3,2,1,0:T(8,128)(2,1)}, bf16[2,2,96,256]{3,2,1,0:T(8,128)(2,1)S(1)}, u32[]{:S(2)}, u32[]{:S(2)}) collective-permute-start(bf16[2,2,96,256]{3,2,1,0:T(8,128)(2,1)} %get-tuple-element.9), channel_id=1, source_target_pairs={{0,1},{1,2},{2,3},{3,4},{4,5},{5,6},{6,7},{7,8},{8,9},{9,10},{10,1... | collective-permute-start | bytes 589832 | tf_op jit(solution)/shard_map/ppermute | solution.py:243
  7.2 1.3 %collective-permute-start.3 = (bf16[2,2,96,256]{3,2,1,0:T(8,128)(2,1)}, bf16[2,2,96,256]{3,2,1,0:T(8,128)(2,1)S(1)}, u32[]{:S(2)}, u32[]{:S(2)}) collective-permute-start(bf16[2,2,96,256]{3,2,1,0:T(8,128)(2,1)} %get-tuple-element.10), channel_id=1, source_target_pairs={{1,0},{2,1},{3,2},{4,3},{5,4},{6,5},{7,6},{8,7},{9,8},{10,9},{11,1... | collective-permute-start | bytes 589832 | tf_op jit(solution)/shard_map/ppermute | solution.py:243
  8.5 3.7 %collective-permute-start = (bf16[2,2,96,256]{3,2,1,0:T(8,128)(2,1)}, bf16[2,2,96,256]{3,2,1,0:T(8,128)(2,1)S(1)}, u32[]{:S(2)}, u32[]{:S(2)}) collective-permute-start(bf16[2,2,96,256]{3,2,1,0:T(8,128)(2,1)} %get-tuple-element.7), channel_id=1, source_target_pairs={{0,16},{16,32},{32,48},{48,64},{64,80},{80,96},{96,112},{1,17},{17... | collective-permute-start | bytes 589832 | tf_op jit(solution)/shard_map/ppermute | solution.py:243
  12.2 1.9 %collective-permute-start.1 = (bf16[2,2,96,256]{3,2,1,0:T(8,128)(2,1)}, bf16[2,2,96,256]{3,2,1,0:T(8,128)(2,1)S(1)}, u32[]{:S(2)}, u32[]{:S(2)}) collective-permute-start(bf16[2,2,96,256]{3,2,1,0:T(8,128)(2,1)} %get-tuple-element.8), channel_id=1, source_target_pairs={{16,0},{32,16},{48,32},{64,48},{80,64},{96,80},{112,96},{17,1},{33... | collective-permute-start | bytes 589832 | tf_op jit(solution)/shard_map/ppermute | solution.py:243
  14.2 1.1 collective-permute-done.3
  15.2 0.8 fusion.4
  16.0 3.4 %collective-permute-done.1 = bf16[2,2,96,256]{3,2,1,0:T(8,128)(2,1)S(1)} collective-permute-done((bf16[2,2,96,256]{3,2,1,0:T(8,128)(2,1)}, bf16[2,2,96,256]{3,2,1,0:T(8,128)(2,1)S(1)}, u32[]{:S(2)}, u32[]{:S(2)}) %collective-permute-start.1) | collective-permute-done | bytes 196640 | tf_op jit(solution)/shard_map/ppermute | solution.py:243
  19.4 0.8 fusion.5
  20.2 24.3 %wgrad.1 = f32[288,896]{1,0:T(8,128)} custom-call(s32[1,1,2]{2,1,0:T(1,128)} %act_ref.7, bf16[2,96,4096]{2,1,0:T(8,128)(2,1)} %bitcast.31, bf16[2,96,4096]{2,1,0:T(8,128)(2,1)} %bitcast.34, bf16[2,2,96,256]{3,2,1,0:T(8,128)(2,1)} %get-tuple-element.14.x_ref, bf16[2,2,96,256]{3,2,1,0:T(8,128)(2,1)} %get-tuple-element.12.y_ref), custom_call_target="tpu_custom_call" | custom-call | tf_op jit(solution)/shard_map/wgrad/pallas_call | solution.py:225
  44.5 1.9 %copy.21 = f32[3,96,864]{2,0,1:T(4,128)S(1)} copy(f32[3,96,864]{2,1,0:T(8,128)} %bitcast.39) | data formatting | bytes 1990656 | tf_op jit(solution)/shard_map/reshape | solution.py:266
  46.4 1.1 %reshape.39 = f32[128,1944]{1,0:T(8,128)S(1)} reshape(f32[96,3,864]{2,1,0:T(4,128)S(1)} %bitcast.38) | data formatting | bytes 1990656 | tf_op jit(solution)/shard_map/reshape | solution.py:266
  47.7 1.2 %copy.19 = f32[16,8,16,128]{3,2,1,0:T(8,128)} copy(f32[16,8,16,128]{3,1,2,0:T(8,128)S(1)} %pad_bitcast_fusion) | data formatting | bytes 2097152
  48.8 10.8 %all-to-all-start = ((f32[128,16,128]{2,1,0:T(8,128)}), f32[128,16,128]{2,1,0:T(8,128)S(1)}, u32[]{:S(2)}, u32[]{:S(2)}) async-start(f32[128,16,128]{2,1,0:T(8,128)} %bitcast.20), calls=%async_computation | async-start | bytes 2097152 | tf_op jit(solution)/shard_map/all_to_all | solution.py:270
  59.6 0.3 copy.9
  59.9 1.1 copy.15
  61.0 0.8 reshape.42
  61.9 0.3 copy.16
  62.2 0.8 reshape.43
  63.0 0.8 pad.11.w_ref
  63.8 0.8 pad.12.w_ref
  64.7 23.2 %conv.2 = bf16[2,96,4096]{2,1,0:T(8,128)(2,1)} custom-call(s32[1,1,2]{2,1,0:T(1,128)} %act_ref.7, bf16[2,96,4096]{2,1,0:T(8,128)(2,1)} %bitcast.32, bf16[2,2,96,256]{3,2,1,0:T(8,128)(2,1)} %get-tuple-element.14.x_ref, bf16[2,2,96,256]{3,2,1,0:T(8,128)(2,1)} %get-tuple-element.12.y_ref, bf16[288,896]{1,0:T(8,128)(2,1)} %pad.11.w_ref), custom_call_target="tpu_custom_call" | custom-call | tf_op jit(solution)/shard_map/conv/pallas_call | solution.py:158
  87.9 23.2 %conv.3 = bf16[2,96,4096]{2,1,0:T(8,128)(2,1)} custom-call(s32[1,1,2]{2,1,0:T(1,128)} %act_ref.7, bf16[2,96,4096]{2,1,0:T(8,128)(2,1)} %bitcast.35, bf16[2,2,96,256]{3,2,1,0:T(8,128)(2,1)} %get-tuple-element.13.x_ref, bf16[2,2,96,256]{3,2,1,0:T(8,128)(2,1)} %get-tuple-element.11.y_ref, bf16[288,896]{1,0:T(8,128)(2,1)} %pad.12.w_ref), custom_call_target="tpu_custom_call" | custom-call | tf_op jit(solution)/shard_map/conv/pallas_call | solution.py:158
  111.2 0.6 slice_multiply_fusion
  (8 shorter events, 0.3 us)
Async XLA Ops:
  3.7 10.5 %collective-permute-start.2 = (bf16[2,2,96,256]{3,2,1,0:T(8,128)(2,1)}, bf16[2,2,96,256]{3,2,1,0:T(8,128)(2,1)S(1)}, u32[]{:S(2)}, u32[]{:S(2)}) collective-permute-start(bf16[2,2,96,256]{3,2,1,0:T(8,128)(2,1)} %get-tuple-element.9), channel_id=1, source_target_pairs={{0,1},{1,2},{2,3},{3,4},{4,5},{5,6},{6,7},{7,8},{8,9},{9,10},{10,1... | collective-permute-start | bytes 589832 | tf_op jit(solution)/shard_map/ppermute | solution.py:243
  7.2 8.0 %collective-permute-start.3 = (bf16[2,2,96,256]{3,2,1,0:T(8,128)(2,1)}, bf16[2,2,96,256]{3,2,1,0:T(8,128)(2,1)S(1)}, u32[]{:S(2)}, u32[]{:S(2)}) collective-permute-start(bf16[2,2,96,256]{3,2,1,0:T(8,128)(2,1)} %get-tuple-element.10), channel_id=1, source_target_pairs={{1,0},{2,1},{3,2},{4,3},{5,4},{6,5},{7,6},{8,7},{9,8},{10,9},{11,1... | collective-permute-start | bytes 589832 | tf_op jit(solution)/shard_map/ppermute | solution.py:243
  8.5 7.5 %collective-permute-start = (bf16[2,2,96,256]{3,2,1,0:T(8,128)(2,1)}, bf16[2,2,96,256]{3,2,1,0:T(8,128)(2,1)S(1)}, u32[]{:S(2)}, u32[]{:S(2)}) collective-permute-start(bf16[2,2,96,256]{3,2,1,0:T(8,128)(2,1)} %get-tuple-element.7), channel_id=1, source_target_pairs={{0,16},{16,32},{32,48},{48,64},{64,80},{80,96},{96,112},{1,17},{17... | collective-permute-start | bytes 589832 | tf_op jit(solution)/shard_map/ppermute | solution.py:243
  12.2 7.2 %collective-permute-start.1 = (bf16[2,2,96,256]{3,2,1,0:T(8,128)(2,1)}, bf16[2,2,96,256]{3,2,1,0:T(8,128)(2,1)S(1)}, u32[]{:S(2)}, u32[]{:S(2)}) collective-permute-start(bf16[2,2,96,256]{3,2,1,0:T(8,128)(2,1)} %get-tuple-element.8), channel_id=1, source_target_pairs={{16,0},{32,16},{48,32},{64,48},{80,64},{96,80},{112,96},{17,1},{33... | collective-permute-start | bytes 589832 | tf_op jit(solution)/shard_map/ppermute | solution.py:243
  48.8 10.8 %copy-start = (bf16[96,2592]{1,0:T(8,128)(2,1)S(1)}, bf16[96,2592]{1,0:T(8,128)(2,1)}, u32[]{:S(2)}) copy-start(bf16[96,2592]{1,0:T(8,128)(2,1)} %param.6) | copy-start | bytes 1492996
  48.8 62.2 %all-to-all-start = ((f32[128,16,128]{2,1,0:T(8,128)}), f32[128,16,128]{2,1,0:T(8,128)S(1)}, u32[]{:S(2)}, u32[]{:S(2)}) async-start(f32[128,16,128]{2,1,0:T(8,128)} %bitcast.20), calls=%async_computation | async-start | bytes 2097152 | tf_op jit(solution)/shard_map/all_to_all | solution.py:270

commit v2 on v1

--- a/solution.py
+++ b/solution.py
@@ -62,54 +62,70 @@
     )(active, features, grads)
 
 
-def shifted_rows(y_ref, lev, ys_ref):
-    c = ys_ref.shape[2]
-    z = lanes_of((c, PLANE)) % EDGE
-    zero = jnp.zeros((c, PLANE), bf16)
-    for side in range(2):
-        row = y_ref[side, lev]
-        ys_ref[side, 0] = pick(z == 0, zero, pltpu.roll(row, 1, 1))
-        ys_ref[side, 1] = row
-        ys_ref[side, 2] = pick(z == EDGE - 1, zero, pltpu.roll(row, PLANE - 1, 1))
-
-
-def fill_plane(store, plane, below, above, rows):
-    c = plane.shape[0]
-    lane = lanes_of((c, PLANE))
+def z_moved(value, mask, fill, amount):
+    return pick(mask, fill, pltpu.roll(value, amount, 1))
+
+
+def fill_plane(store, halves, fills, edge):
+    c = halves[0].shape[0]
+    lane = lanes_of((c, 128))
     z = lane % EDGE
-    down = pltpu.roll(pick(z == EDGE - 1, pltpu.roll(below, PLANE - EDGE, 1), plane), 1, 1)
-    up = pltpu.roll(pick(z == 0, pltpu.roll(above, EDGE, 1), plane), PLANE - 1, 1)
-    for k, value in enumerate((down, plane, up)):
-        south, north = rows(k)
-        store(3 + k, value)
-        store(k, pltpu.roll(pick(lane >= PLANE - EDGE, south, value), EDGE, 1))
-        store(6 + k, pltpu.roll(pick(lane < EDGE, north, value), PLANE - EDGE, 1))
-
-
-def build_inner(store, act_ref, src_ref, ys_ref, lev, x):
+    zero = jnp.zeros((c, 128), bf16)
+    below, above = fills
+    moved = (
+        [z_moved(v, z == 0, f, 1) for v, f in zip(halves, below)],
+        halves,
+        [z_moved(v, z == EDGE - 1, f, 127) for v, f in zip(halves, above)],
+    )
+    if edge is None:
+        rows = (zero,) * 3
+    else:
+        rows = (z_moved(edge, z == 0, zero, 1), edge, z_moved(edge, z == EDGE - 1, zero, 127))
+    for k in range(3):
+        first, last = moved[k]
+        store(3 + k, 0, first)
+        store(3 + k, 1, last)
+        first_on, last_on = pltpu.roll(first, EDGE, 1), pltpu.roll(last, EDGE, 1)
+        store(k, 0, pick(lane < EDGE, rows[k], first_on))
+        store(k, 1, pick(lane < EDGE, first_on, last_on))
+        first_off, last_off = (pltpu.roll(v, 128 - EDGE, 1) for v in (first, last))
+        store(6 + k, 0, pick(lane >= 128 - EDGE, last_off, first_off))
+        store(6 + k, 1, pick(lane >= 128 - EDGE, rows[k], last_off))
+
+
+def build_inner(store, act_ref, src_ref, y_ref, lev, x):
     c = src_ref.shape[1]
     other = 1 - lev
-    live = act_ref[0, 0, other].astype(f32)
+    live = act_ref[0, 0, other]
     start = pl.multiple_of(x * PLANE, PLANE)
-    plane = src_ref[lev, :, pl.ds(start, PLANE)]
-    beside = src_ref[other, :, pl.ds(start, PLANE)]
-    below = beside * (live * lev.astype(f32)).astype(bf16)
-    above = beside * (live * other.astype(f32)).astype(bf16)
-
-    def rows(k):
-        south = pltpu.roll(ys_ref[0, k], lax.rem(PLANE - EDGE - x * EDGE + PLANE, PLANE), 1)
-        north = pltpu.roll(ys_ref[1, k], lax.rem(PLANE - x * EDGE, PLANE), 1)
-        return south, north
-
-    fill_plane(store, plane, below, above, rows)
+    halves = [src_ref[lev, :, pl.ds(start + h, 128)] for h in (0, 128)]
+    turn = EDGE - 1 + lev * (128 - 2 * (EDGE - 1))
+    beside = [pltpu.roll(src_ref[other, :, pl.ds(start + h, 128)], turn, 1) for h in (0, 128)]
+    below_on = (live * lev).astype(f32).astype(bf16)
+    above_on = (live * other).astype(f32).astype(bf16)
+    below = [v * below_on for v in beside]
+    above = [v * above_on for v in beside]
+    at = pl.multiple_of((x // 8) * 128, 128)
+    back = 16 * lax.rem(x, 8)
+    south = pltpu.roll(y_ref[0, lev, :, pl.ds(at, 128)], lax.rem(128 - back, 128), 1)
+    north = pltpu.roll(y_ref[1, lev, :, pl.ds(at, 128)], 112 - back, 1)
+    edge = pick(lanes_of((c, 128)) < EDGE, south, north)
+    fill_plane(store, halves, (below, above), edge)
 
 
 def build_outer(store, plane):
-    zero = jnp.zeros_like(plane)
-    fill_plane(store, plane, zero, zero, lambda k: (zero, zero))
-
-
-def conv_kernel(act_ref, src_ref, x_ref, y_ref, w_ref, out_ref, p_ref, ys_ref, acc_ref):
+    zero = jnp.zeros((plane.shape[0], 128), bf16)
+    fill_plane(store, [plane[:, :128], plane[:, 128:]], ([zero] * 2,) * 2, None)
+
+
+def storing(p_ref, c, start=0):
+    def store(at, half, value):
+        p_ref[at * c : (at + 1) * c, start + half * 128 : start + half * 128 + 128] = value
+
+    return store
+
+
+def conv_kernel(act_ref, src_ref, x_ref, y_ref, w_ref, out_ref, pa_ref, pb_ref, acc_ref):
     lev = pl.program_id(0)
     c = src_ref.shape[1]
 
@@ -119,36 +135,37 @@
 
     @pl.when(act_ref[0, 0, lev] != 0)
     def _():
-        p_ref[NEAR * c :] = jnp.zeros_like(p_ref[NEAR * c :])
-        shifted_rows(y_ref, lev, ys_ref)
-
-        def store(at, value):
-            p_ref[at * c : (at + 1) * c] = value
-
-        def product():
+        def inner(p_ref, x):
+            build_inner(storing(p_ref, c), act_ref, src_ref, y_ref, lev, x)
+
+        def product(p_ref):
             return jnp.dot(w_ref[...], p_ref[...], preferred_element_type=f32)
 
-        build_outer(store, x_ref[0, lev])
-        acc_ref[0] = product()[:c]
-        acc_ref[1] = jnp.zeros_like(acc_ref[1])
-
-        def step(x, _):
-            build_inner(store, act_ref, src_ref, ys_ref, lev, x)
-            full = product()
+        def advance(p_ref, x):
+            full = product(p_ref)
             done = acc_ref[1] + full[2 * c :]
             acc_ref[1] = acc_ref[0] + full[c : 2 * c]
             acc_ref[0] = full[:c]
-
-            @pl.when(x > 0)
-            def _():
-                out_ref[:, pl.ds(pl.multiple_of((x - 1) * PLANE, PLANE), PLANE)] = done.astype(bf16)
-
+            start = pl.multiple_of(jnp.maximum(x - 1, 0) * PLANE, PLANE)
+            out_ref[:, pl.ds(start, PLANE)] = done.astype(bf16)
+
+        for p_ref in (pa_ref, pb_ref):
+            p_ref[NEAR * c :] = jnp.zeros_like(p_ref[NEAR * c :])
+        acc_ref[...] = jnp.zeros_like(acc_ref)
+        build_outer(storing(pa_ref, c), x_ref[0, lev])
+
+        def step(j, _):
+            x = 2 * j
+            inner(pb_ref, x)
+            advance(pa_ref, x - 1)
+            inner(pa_ref, x + 1)
+            advance(pb_ref, x)
             return 0
 
-        lax.fori_loop(0, EDGE, step, 0)
-        build_outer(store, x_ref[1, lev])
-        full = product()
-        out_ref[:, 15 * PLANE :] = (acc_ref[1] + full[2 * c :]).astype(bf16)
+        lax.fori_loop(0, EDGE // 2, step, 0)
+        build_outer(storing(pb_ref, c), x_ref[1, lev])
+        advance(pa_ref, EDGE - 1)
+        advance(pb_ref, EDGE)
 
 
 def conv(active, src, xface, yface, weight):
@@ -163,55 +180,66 @@
         out_shape=jax.ShapeDtypeStruct((levels, c, vox), bf16),
         scratch_shapes=[
             pltpu.VMEM((depth, PLANE), bf16),
-            pltpu.VMEM((2, 3, c, PLANE), bf16),
+            pltpu.VMEM((depth, PLANE), bf16),
             pltpu.VMEM((2, c, PLANE), f32),
         ],
         name="conv",
     )(active, src, xface, yface, weight)
 
 
-def wgrad_kernel(act_ref, src_ref, grad_ref, x_ref, y_ref, out_ref, p_ref, g_ref, ys_ref):
+CHUNK = 3
+
+
+def wgrad_kernel(act_ref, src_ref, grad_ref, x_ref, y_ref, out_ref, pa_ref, pb_ref, g_ref):
     c = src_ref.shape[1]
-    planes = EDGE + 2
-
+    chunks = (EDGE + 2) // CHUNK
+    wide = CHUNK * PLANE
     out_ref[...] = jnp.zeros_like(out_ref)
-    p_ref[NEAR * c :] = jnp.zeros_like(p_ref[NEAR * c :])
-    g_ref[...] = jnp.zeros_like(g_ref)
+    for p_ref in (pa_ref, pb_ref):
+        p_ref[NEAR * c :] = jnp.zeros_like(p_ref[NEAR * c :])
+    g_ref[:, : 2 * PLANE] = jnp.zeros((c, 2 * PLANE), bf16)
+    g_ref[:, (EDGE + 2) * PLANE :] = jnp.zeros((c, 2 * PLANE), bf16)
 
     def level(lev, _):
         @pl.when(act_ref[0, 0, lev] != 0)
         def _():
-            shifted_rows(y_ref, lev, ys_ref)
-
-            def store_at(start):
-                def store(at, value):
-                    p_ref[at * c : (at + 1) * c, pl.ds(start, PLANE)] = value
-
-                return store
-
-            for dx in range(3):
-                g_ref[dx * c : (dx + 1) * c, dx * PLANE : (dx + EDGE) * PLANE] = grad_ref[lev]
-            build_outer(store_at(0), x_ref[0, lev])
-
-            def step(x, _):
-                start = pl.multiple_of((x + 1) * PLANE, PLANE)
-                build_inner(store_at(start), act_ref, src_ref, ys_ref, lev, x)
-                return 0
-
-            lax.fori_loop(0, EDGE, step, 0)
-            build_outer(store_at((EDGE + 1) * PLANE), x_ref[1, lev])
-
-            def gather(at, _):
-                cells = pl.ds(pl.multiple_of(at * 3 * PLANE, 3 * PLANE), 3 * PLANE)
+            g_ref[:, 2 * PLANE : (EDGE + 2) * PLANE] = grad_ref[lev]
+
+            def fill(p_ref, at, first=False, last=False):
+                for n in range(CHUNK):
+                    store = storing(p_ref, c, n * PLANE)
+                    if first and n == 0:
+                        build_outer(store, x_ref[0, lev])
+                    elif last and n == CHUNK - 1:
+                        build_outer(store, x_ref[1, lev])
+                    else:
+                        build_inner(store, act_ref, src_ref, y_ref, lev, at * CHUNK + n - 1)
+
+            def gather(p_ref, at):
+                moved = [
+                    g_ref[:, pl.ds(pl.multiple_of((at * CHUNK + 2 - dx) * PLANE, PLANE), wide)]
+                    for dx in range(3)
+                ]
                 out_ref[...] += lax.dot_general(
-                    g_ref[:, cells],
-                    p_ref[:, cells],
+                    jnp.concatenate(moved, axis=0),
+                    p_ref[...],
                     (((1,), (1,)), ((), ())),
                     preferred_element_type=f32,
                 )
+
+            fill(pa_ref, jnp.int32(0), first=True)
+
+            def step(j, _):
+                fill(pb_ref, 2 * j + 1)
+                gather(pa_ref, 2 * j)
+                fill(pa_ref, 2 * j + 2)
+                gather(pb_ref, 2 * j + 1)
                 return 0
 
-            lax.fori_loop(0, planes // 3, gather, 0)
+            lax.fori_loop(0, chunks // 2 - 1, step, 0)
+            fill(pb_ref, jnp.int32(chunks - 1), last=True)
+            gather(pa_ref, jnp.int32(chunks - 2))
+            gather(pb_ref, jnp.int32(chunks - 1))
 
         return 0
 
@@ -221,16 +249,15 @@
 def wgrad(active, src, grads, xface, yface, depth):
     levels, c, vox = src.shape
     whole = pl.BlockSpec(memory_space=pltpu.VMEM)
-    wide = (EDGE + 2) * PLANE
     return pl.pallas_call(
         wgrad_kernel,
         in_specs=[pl.BlockSpec(memory_space=pltpu.SMEM)] + [whole] * 4,
         out_specs=whole,
         out_shape=jax.ShapeDtypeStruct((3 * c, depth), f32),
         scratch_shapes=[
-            pltpu.VMEM((depth, wide), bf16),
-            pltpu.VMEM((3 * c, wide), bf16),
-            pltpu.VMEM((2, 3, c, PLANE), bf16),
+            pltpu.VMEM((depth, CHUNK * PLANE), bf16),
+            pltpu.VMEM((depth, CHUNK * PLANE), bf16),
+            pltpu.VMEM((c, (EDGE + 4) * PLANE), bf16),
         ],
         name="wgrad",
     )(active, src, grads, xface, yface)

time: 112 us -> 82.7 us (0.74)
  the two profiles are of different devices: /device:TPU:5 before, /device:TPU:1 now
where the time goes in v2:
time: 82.7 us; the launch traced here: 82.4 us
  Pallas kernels  43.6 us (53%)
  starting transfers between devices  21.9 us (26%)
  local copies, waits for them, and re-layouts  9.32 us (11%)
  waiting for transfers between devices  4.47 us (5%)
  other arithmetic  2.31 us (3%)
    pallas_call x2, Pallas kernels, conv(): pl.pallas_call(conv_kernel, grid=(levels,), in_specs=[pl.BlockSpec(memory...  29.1 us
    pallas_call x1, Pallas kernels, wgrad(): pl.pallas_call(wgrad_kernel, in_specs=[pl.BlockSpec(memory_space=pltpu.SM...  11.5 us
    all_to_all x1, starting transfers between devices, body(): swapped = lax.all_to_all(flat, ('gx', 'gy'), 0, 0, tiled=True)  10.4 us
    ppermute x2, starting transfers between devices, neighbours(): lax.ppermute(high, axis, forward)  8.32 us
    ppermute x2, waiting for transfers between devices, neighbours(): lax.ppermute(low, axis, backward)  4.46 us
    ppermute x2, starting transfers between devices, neighbours(): lax.ppermute(low, axis, backward)  3.21 us
    reshape x2, local copies, waits for them, and re-layouts, body(): gw[:, :NEAR * c].reshape(3, c, NEAR * c).transpose(1, 0, 2)  3.07 us
    pallas_call x1, Pallas kernels, pack(): pl.pallas_call(pack_kernel, grid=(levels,), in_specs=[pl.BlockSpec(memory...  3.06 us
  transfers between devices with their start and end apart: 5, of which 2 were waited for; matrix products, arithmetic and copies ran while one was open for 7% of the time, Pallas kernels for 35%

profile of v2, /device:TPU:1, one launch (start us, length us, event | category | flops | bytes accessed | tf_op | source)
XLA Modules:
  0.0 82.4 jit_solution(15641079270232826257)
XLA Ops:
  0.6 3.1 %pack_faces.1 = (bf16[2,2,96,256]{3,2,1,0:T(8,128)(2,1)}, bf16[2,2,96,256]{3,2,1,0:T(8,128)(2,1)}, bf16[2,2,96,256]{3,2,1,0:T(8,128)(2,1)}, bf16[2,2,96,256]{3,2,1,0:T(8,128)(2,1)}) custom-call(s32[1,1,2]{2,1,0:T(1,128)} %act_ref.7, bf16[2,96,4096]{2,1,0:T(8,128)(2,1)} %bitcast.30, bf16[2,96,4096]{2,1,0:T(8,128)(2,1)} %bitcast.33), custom_call_target="tpu_custom_call" | custom-call | tf_op jit(solution)/shard_map/pack_faces/pallas_call | solution.py:55
  3.7 4.4 %collective-permute-start.2 = (bf16[2,2,96,256]{3,2,1,0:T(8,128)(2,1)}, bf16[2,2,96,256]{3,2,1,0:T(8,128)(2,1)S(1)}, u32[]{:S(2)}, u32[]{:S(2)}) collective-permute-start(bf16[2,2,96,256]{3,2,1,0:T(8,128)(2,1)} %get-tuple-element.9), channel_id=1, source_target_pairs={{0,1},{1,2},{2,3},{3,4},{4,5},{5,6},{6,7},{7,8},{8,9},{9,10},{10,1... | collective-permute-start | bytes 589832 | tf_op jit(solution)/shard_map/ppermute | solution.py:270
  8.1 1.3 %collective-permute-start.3 = (bf16[2,2,96,256]{3,2,1,0:T(8,128)(2,1)}, bf16[2,2,96,256]{3,2,1,0:T(8,128)(2,1)S(1)}, u32[]{:S(2)}, u32[]{:S(2)}) collective-permute-start(bf16[2,2,96,256]{3,2,1,0:T(8,128)(2,1)} %get-tuple-element.10), channel_id=1, source_target_pairs={{1,0},{2,1},{3,2},{4,3},{5,4},{6,5},{7,6},{8,7},{9,8},{10,9},{11,1... | collective-permute-start | bytes 589832 | tf_op jit(solution)/shard_map/ppermute | solution.py:270
  9.4 4.0 %collective-permute-start = (bf16[2,2,96,256]{3,2,1,0:T(8,128)(2,1)}, bf16[2,2,96,256]{3,2,1,0:T(8,128)(2,1)S(1)}, u32[]{:S(2)}, u32[]{:S(2)}) collective-permute-start(bf16[2,2,96,256]{3,2,1,0:T(8,128)(2,1)} %get-tuple-element.7), channel_id=1, source_target_pairs={{0,16},{16,32},{32,48},{48,64},{64,80},{80,96},{96,112},{1,17},{17... | collective-permute-start | bytes 589832 | tf_op jit(solution)/shard_map/ppermute | solution.py:270
  13.3 1.9 %collective-permute-start.1 = (bf16[2,2,96,256]{3,2,1,0:T(8,128)(2,1)}, bf16[2,2,96,256]{3,2,1,0:T(8,128)(2,1)S(1)}, u32[]{:S(2)}, u32[]{:S(2)}) collective-permute-start(bf16[2,2,96,256]{3,2,1,0:T(8,128)(2,1)} %get-tuple-element.8), channel_id=1, source_target_pairs={{16,0},{32,16},{48,32},{64,48},{80,64},{96,80},{112,96},{17,1},{33... | collective-permute-start | bytes 589832 | tf_op jit(solution)/shard_map/ppermute | solution.py:270
  15.3 0.8 collective-permute-done.3
  16.0 0.8 fusion.4
  16.8 3.7 %collective-permute-done.1 = bf16[2,2,96,256]{3,2,1,0:T(8,128)(2,1)S(1)} collective-permute-done((bf16[2,2,96,256]{3,2,1,0:T(8,128)(2,1)}, bf16[2,2,96,256]{3,2,1,0:T(8,128)(2,1)S(1)}, u32[]{:S(2)}, u32[]{:S(2)}) %collective-permute-start.1) | collective-permute-done | bytes 196640 | tf_op jit(solution)/shard_map/ppermute | solution.py:270
  20.5 0.8 fusion.5
  21.3 11.5 %wgrad.1 = f32[288,896]{1,0:T(8,128)} custom-call(s32[1,1,2]{2,1,0:T(1,128)} %act_ref.7, bf16[2,96,4096]{2,1,0:T(8,128)(2,1)} %bitcast.31, bf16[2,96,4096]{2,1,0:T(8,128)(2,1)} %bitcast.34, bf16[2,2,96,256]{3,2,1,0:T(8,128)(2,1)} %get-tuple-element.14.x_ref, bf16[2,2,96,256]{3,2,1,0:T(8,128)(2,1)} %get-tuple-element.12.y_ref), custom_call_target="tpu_custom_call" | custom-call | tf_op jit(solution)/shard_map/wgrad/pallas_call | solution.py:252
  32.8 1.9 %copy.21 = f32[3,96,864]{2,0,1:T(4,128)S(1)} copy(f32[3,96,864]{2,1,0:T(8,128)} %bitcast.39) | data formatting | bytes 1990656 | tf_op jit(solution)/shard_map/reshape | solution.py:293
  34.7 1.1 %reshape.39 = f32[128,1944]{1,0:T(8,128)S(1)} reshape(f32[96,3,864]{2,1,0:T(4,128)S(1)} %bitcast.38) | data formatting | bytes 1990656 | tf_op jit(solution)/shard_map/reshape | solution.py:293
  35.9 1.2 %copy.19 = f32[16,8,16,128]{3,2,1,0:T(8,128)} copy(f32[16,8,16,128]{3,1,2,0:T(8,128)S(1)} %pad_bitcast_fusion) | data formatting | bytes 2097152
  37.1 10.4 %all-to-all-start = ((f32[128,16,128]{2,1,0:T(8,128)}), f32[128,16,128]{2,1,0:T(8,128)S(1)}, u32[]{:S(2)}, u32[]{:S(2)}) async-start(f32[128,16,128]{2,1,0:T(8,128)} %bitcast.20), calls=%async_computation | async-start | bytes 2097152 | tf_op jit(solution)/shard_map/all_to_all | solution.py:297
  47.5 0.3 copy.9
  47.8 1.1 %copy.15 = bf16[3,96,9,96]{3,2,1,0:T(8,128)(2,1)S(1)} copy(bf16[3,96,9,96]{1,3,2,0:T(8,128)(2,1)S(1)} %bitcast.36) | data formatting | bytes 995328 | tf_op jit(solution)/shard_map/reshape | solution.py:286
  48.9 0.8 reshape.42
  49.7 0.3 copy.16
  50.1 0.8 reshape.43
  50.9 0.8 %pad.11.w_ref = bf16[288,896]{1,0:T(8,128)(2,1)} pad(bf16[288,864]{1,0:T(8,128)(2,1)S(1)} %reshape.42, bf16[]{:T(256)} %constant.2.clone.1), padding=0_0x0_32 | pad | bytes 1013762 | tf_op jit(solution)/shard_map/jit(_pad)/pad | solution.py:286
  51.7 0.8 %pad.12.w_ref = bf16[288,896]{1,0:T(8,128)(2,1)} pad(bf16[288,864]{1,0:T(8,128)(2,1)S(1)} %reshape.43, bf16[]{:T(256)} %constant.2.clone.1), padding=0_0x0_32 | pad | bytes 1013762 | tf_op jit(solution)/shard_map/jit(_pad)/pad | solution.py:287
  52.5 14.5 %conv.2 = bf16[2,96,4096]{2,1,0:T(8,128)(2,1)} custom-call(s32[1,1,2]{2,1,0:T(1,128)} %act_ref.7, bf16[2,96,4096]{2,1,0:T(8,128)(2,1)} %bitcast.32, bf16[2,2,96,256]{3,2,1,0:T(8,128)(2,1)} %get-tuple-element.14.x_ref, bf16[2,2,96,256]{3,2,1,0:T(8,128)(2,1)} %get-tuple-element.12.y_ref, bf16[288,896]{1,0:T(8,128)(2,1)} %pad.11.w_ref), custom_call_target="tpu_custom_call" | custom-call | tf_op jit(solution)/shard_map/conv/pallas_call | solution.py:175
  67.1 14.5 %conv.3 = bf16[2,96,4096]{2,1,0:T(8,128)(2,1)} custom-call(s32[1,1,2]{2,1,0:T(1,128)} %act_ref.7, bf16[2,96,4096]{2,1,0:T(8,128)(2,1)} %bitcast.35, bf16[2,2,96,256]{3,2,1,0:T(8,128)(2,1)} %get-tuple-element.13.x_ref, bf16[2,2,96,256]{3,2,1,0:T(8,128)(2,1)} %get-tuple-element.11.y_ref, bf16[288,896]{1,0:T(8,128)(2,1)} %pad.12.w_ref), custom_call_target="tpu_custom_call" | custom-call | tf_op jit(solution)/shard_map/conv/pallas_call | solution.py:175
  81.8 0.6 slice_multiply_fusion
  (8 shorter events, 0.3 us)
Async XLA Ops:
  3.7 11.6 %collective-permute-start.2 = (bf16[2,2,96,256]{3,2,1,0:T(8,128)(2,1)}, bf16[2,2,96,256]{3,2,1,0:T(8,128)(2,1)S(1)}, u32[]{:S(2)}, u32[]{:S(2)}) collective-permute-start(bf16[2,2,96,256]{3,2,1,0:T(8,128)(2,1)} %get-tuple-element.9), channel_id=1, source_target_pairs={{0,1},{1,2},{2,3},{3,4},{4,5},{5,6},{6,7},{7,8},{8,9},{9,10},{10,1... | collective-permute-start | bytes 589832 | tf_op jit(solution)/shard_map/ppermute | solution.py:270
  8.1 8.0 %collective-permute-start.3 = (bf16[2,2,96,256]{3,2,1,0:T(8,128)(2,1)}, bf16[2,2,96,256]{3,2,1,0:T(8,128)(2,1)S(1)}, u32[]{:S(2)}, u32[]{:S(2)}) collective-permute-start(bf16[2,2,96,256]{3,2,1,0:T(8,128)(2,1)} %get-tuple-element.10), channel_id=1, source_target_pairs={{1,0},{2,1},{3,2},{4,3},{5,4},{6,5},{7,6},{8,7},{9,8},{10,9},{11,1... | collective-permute-start | bytes 589832 | tf_op jit(solution)/shard_map/ppermute | solution.py:270
  9.4 7.5 %collective-permute-start = (bf16[2,2,96,256]{3,2,1,0:T(8,128)(2,1)}, bf16[2,2,96,256]{3,2,1,0:T(8,128)(2,1)S(1)}, u32[]{:S(2)}, u32[]{:S(2)}) collective-permute-start(bf16[2,2,96,256]{3,2,1,0:T(8,128)(2,1)} %get-tuple-element.7), channel_id=1, source_target_pairs={{0,16},{16,32},{32,48},{48,64},{64,80},{80,96},{96,112},{1,17},{17... | collective-permute-start | bytes 589832 | tf_op jit(solution)/shard_map/ppermute | solution.py:270
  13.3 7.2 %collective-permute-start.1 = (bf16[2,2,96,256]{3,2,1,0:T(8,128)(2,1)}, bf16[2,2,96,256]{3,2,1,0:T(8,128)(2,1)S(1)}, u32[]{:S(2)}, u32[]{:S(2)}) collective-permute-start(bf16[2,2,96,256]{3,2,1,0:T(8,128)(2,1)} %get-tuple-element.8), channel_id=1, source_target_pairs={{16,0},{32,16},{48,32},{64,48},{80,64},{96,80},{112,96},{17,1},{33... | collective-permute-start | bytes 589832 | tf_op jit(solution)/shard_map/ppermute | solution.py:270
  37.1 10.4 %copy-start = (bf16[96,2592]{1,0:T(8,128)(2,1)S(1)}, bf16[96,2592]{1,0:T(8,128)(2,1)}, u32[]{:S(2)}) copy-start(bf16[96,2592]{1,0:T(8,128)(2,1)} %param.6) | copy-start | bytes 1492996
  37.1 44.5 %all-to-all-start = ((f32[128,16,128]{2,1,0:T(8,128)}), f32[128,16,128]{2,1,0:T(8,128)S(1)}, u32[]{:S(2)}, u32[]{:S(2)}) async-start(f32[128,16,128]{2,1,0:T(8,128)} %bitcast.20), calls=%async_computation | async-start | bytes 2097152 | tf_op jit(solution)/shard_map/all_to_all | solution.py:297

commit v3 on v2

v3 whole, which is shorter than its diff:
```python
import functools
import math

import jax
import jax.numpy as jnp
from jax import lax
from jax.experimental import pallas as pl
from jax.experimental.pallas import tpu as pltpu
from jax.sharding import PartitionSpec as P

EDGE = 16
CONV_CHUNK = 3
CHUNK = 4
PLANE = EDGE * EDGE
NEAR = 9
bf16 = jnp.bfloat16
f32 = jnp.float32


def lanes_of(shape):
    return lax.broadcasted_iota(jnp.int32, shape, 1)


def pick(mask, a, b):
    return jnp.where(mask, a, b)


def pack_kernel(act_ref, f_ref, g_ref, xlo_ref, xhi_ref, ylo_ref, yhi_ref):
    c = f_ref.shape[0]
    live = act_ref[0, 0, pl.program_id(0)].astype(f32).astype(bf16)
    half = lanes_of((c, 128)) // EDGE
    for arr, src in enumerate((f_ref, g_ref)):
        xlo_ref[arr] = src[:, 0:PLANE] * live
        xhi_ref[arr] = src[:, 15 * PLANE : 16 * PLANE] * live
        for h in range(2):
            low = jnp.zeros((c, 128), bf16)
            high = jnp.zeros((c, 128), bf16)
            for xs in range(8):
                x = 8 * h + xs
                a = src[:, x * PLANE : x * PLANE + 128]
                b = src[:, x * PLANE + 128 : x * PLANE + 256]
                if xs:
                    a = pltpu.roll(a, 16 * xs, 1)
                if xs != 7:
                    b = pltpu.roll(b, 16 * xs + 16, 1)
                low = pick(half == xs, a, low)
                high = pick(half == xs, b, high)
            ylo_ref[arr, :, h * 128 : h * 128 + 128] = low * live
            yhi_ref[arr, :, h * 128 : h * 128 + 128] = high * live


def pack(active, features, grads):
    levels, c, vox = features.shape
    face = jax.ShapeDtypeStruct((2, levels, c, PLANE), bf16)
    brick = pl.BlockSpec((None, c, vox), lambda k: (k, 0, 0))
    side = pl.BlockSpec((2, None, c, PLANE), lambda k: (0, k, 0, 0))
    return pl.pallas_call(
        pack_kernel,
        grid=(levels,),
        in_specs=[pl.BlockSpec(memory_space=pltpu.SMEM), brick, brick],
        out_specs=[side] * 4,
        out_shape=[face] * 4,
        name="pack_faces",
    )(active, features, grads)


def turned(value, amount):
    return pltpu.roll(value, amount % 128, 1) if amount % 128 else value


def z_moved(value, mask, fill, amount):
    return pick(mask, fill, pltpu.roll(value, amount, 1))


def fill_plane(store, halves, fills, edge):
    c = halves[0].shape[0]
    lane = lanes_of((c, 128))
    z = lane % EDGE
    zero = jnp.zeros((c, 128), bf16)
    below, above = fills
    moved = (
        [z_moved(v, z == 0, f, 1) for v, f in zip(halves, below)],
        halves,
        [z_moved(v, z == EDGE - 1, f, 127) for v, f in zip(halves, above)],
    )
    if edge is None:
        rows = (zero,) * 3
    else:
        rows = (z_moved(edge, z == 0, zero, 1), edge, z_moved(edge, z == EDGE - 1, zero, 127))
    for k in range(3):
        first, last = moved[k]
        store(3 + k, 0, first)
        store(3 + k, 1, last)
        first_on, last_on = pltpu.roll(first, EDGE, 1), pltpu.roll(last, EDGE, 1)
        store(k, 0, pick(lane < EDGE, rows[k], first_on))
        store(k, 1, pick(lane < EDGE, first_on, last_on))
        first_off, last_off = (pltpu.roll(v, 128 - EDGE, 1) for v in (first, last))
        store(6 + k, 0, pick(lane >= 128 - EDGE, last_off, first_off))
        store(6 + k, 1, pick(lane >= 128 - EDGE, rows[k], last_off))


def build_inner(store, act_ref, src_ref, y_refs, arr, lev, x):
    c = src_ref.shape[1]
    other = 1 - lev
    live = act_ref[0, 0, other]
    start = x * PLANE
    halves = [src_ref[lev, :, pl.ds(start + h, 128)] for h in (0, 128)]
    turn = EDGE - 1 + lev * (128 - 2 * (EDGE - 1))
    beside = [pltpu.roll(src_ref[other, :, pl.ds(start + h, 128)], turn, 1) for h in (0, 128)]
    below_on = (live * lev).astype(f32).astype(bf16)
    above_on = (live * other).astype(f32).astype(bf16)
    below = [v * below_on for v in beside]
    above = [v * above_on for v in beside]
    edge = None
    if y_refs is not None:
        at = (x // 8) * 128
        back = EDGE * (x % 8)
        south, north = (r[arr, lev, :, at : at + 128] for r in y_refs)
        south, north = turned(south, -back), turned(north, 112 - back)
        edge = pick(lanes_of((c, 128)) < EDGE, south, north)
    fill_plane(store, halves, (below, above), edge)


def build_outer(store, plane):
    zero = jnp.zeros((plane.shape[0], 128), bf16)
    fill_plane(store, [plane[:, :128], plane[:, 128:]], ([zero] * 2,) * 2, None)


def storing(p_ref, c, start=0):
    def store(at, half, value):
        p_ref[at * c : (at + 1) * c, start + half * 128 : start + half * 128 + 128] = value

    return store


def conv_kernel(
    act_ref, f_ref, g_ref, xw_ref, xe_ref, ys_ref, yn_ref, w_ref, out_ref, back_ref,
    src_ref, pa_ref, pb_ref, acc_ref, res_ref, in_sem, out_sem,
):
    c = src_ref.shape[2]
    levels = src_ref.shape[1]
    chunks = (EDGE + 2) // CONV_CHUNK
    loads = [pltpu.make_async_copy(r, src_ref.at[i], in_sem.at[i]) for i, r in enumerate((f_ref, g_ref))]
    for load in loads:
        load.start()
    bufs = (pa_ref, pb_ref)
    for p_ref in bufs:
        p_ref[NEAR * c :] = jnp.zeros_like(p_ref[NEAR * c :])

    def save(arr, lev, start):
        slot = lax.rem(lev, 2)
        for i, to in enumerate((out_ref, back_ref)):

            @pl.when(arr == i)
            def _():
                copy = pltpu.make_async_copy(res_ref.at[slot], to.at[lev], out_sem.at[slot])
                copy.start() if start else copy.wait()

    def brick(item, _):
        arr, lev = item // levels, lax.rem(item, levels)
        slot = lax.rem(lev, 2)

        for i, load in enumerate(loads):

            @pl.when(item == i * levels)
            def _():
                load.wait()

        @pl.when(item >= 2)
        def _():
            save((item - 2) // levels, lax.rem(item - 2, levels), False)

        @pl.when(act_ref[0, 0, lev] == 0)
        def _():
            res_ref[slot] = jnp.zeros_like(res_ref[slot])

        @pl.when(act_ref[0, 0, lev] != 0)
        def _():
            def fill(p_ref, at):
                for n in range(CONV_CHUNK):
                    x = at * CONV_CHUNK + n - 1
                    store = storing(p_ref, c, n * PLANE)
                    if x < 0 or x == EDGE:
                        build_outer(store, (xw_ref if x < 0 else xe_ref)[arr, lev])
                    else:
                        build_inner(store, act_ref, src_ref.at[arr], (ys_ref, yn_ref), arr, lev, x)

            def advance(p_ref, at):
                full = jnp.dot(w_ref[arr], p_ref[...], preferred_element_type=f32)
                held = [acc_ref[0], acc_ref[1], None] if at else [None] * 3
                for n in range(CONV_CHUNK):
                    x = at * CONV_CHUNK + n - 1
                    lanes = slice(n * PLANE, (n + 1) * PLANE)
                    for dx in range(3):
                        term = full[dx * c : (dx + 1) * c, lanes]
                        i = 2 - dx
                        held[i] = term if held[i] is None else held[i] + term
                    if x > 0:
                        res_ref[slot, :, (x - 1) * PLANE : x * PLANE] = held[0].astype(bf16)
                    held = held[1:] + [None]
                acc_ref[0] = held[0]
                acc_ref[1] = held[1]

            fill(bufs[0], 0)
            for at in range(chunks):
                if at + 1 < chunks:
                    fill(bufs[(at + 1) % 2], at + 1)
                advance(bufs[at % 2], at)

        save(arr, lev, True)
        return 0

    lax.fori_loop(0, 2 * levels, brick, 0)
    for lev in range(levels - 2, levels):
        save(1, lev, False)


def conv(active, fields, grads, faces, weights):
    levels, c, vox = fields.shape
    depth = weights.shape[2]
    whole = pl.BlockSpec(memory_space=pltpu.VMEM)
    apart = pl.BlockSpec(memory_space=pl.ANY)
    return pl.pallas_call(
        conv_kernel,
        in_specs=[pl.BlockSpec(memory_space=pltpu.SMEM)] + [apart] * 2 + [whole] * 5,
        out_specs=[apart] * 2,
        out_shape=[jax.ShapeDtypeStruct((levels, c, vox), bf16)] * 2,
        scratch_shapes=[
            pltpu.VMEM((2, levels, c, vox), bf16),
            pltpu.VMEM((depth, CONV_CHUNK * PLANE), bf16),
            pltpu.VMEM((depth, CONV_CHUNK * PLANE), bf16),
            pltpu.VMEM((2, c, PLANE), f32),
            pltpu.VMEM((2, c, vox), bf16),
            pltpu.SemaphoreType.DMA((2,)),
            pltpu.SemaphoreType.DMA((2,)),
        ],
        name="conv",
    )(active, fields, grads, *faces, weights)


def wgrad_kernel(act_ref, src_ref, grad_ref, out_ref, pa_ref, pb_ref, g_ref):
    c = src_ref.shape[1]
    chunks = EDGE // CHUNK
    wide = CHUNK * PLANE
    out_ref[...] = jnp.zeros_like(out_ref)
    bufs = (pa_ref, pb_ref)
    for p_ref in bufs:
        p_ref[NEAR * c :] = jnp.zeros_like(p_ref[NEAR * c :])
    g_ref[:, :PLANE] = jnp.zeros((c, PLANE), bf16)
    g_ref[:, (EDGE + 1) * PLANE :] = jnp.zeros((c, PLANE), bf16)

    def level(lev, _):
        @pl.when(act_ref[0, 0, lev] != 0)
        def _():
            g_ref[:, PLANE : (EDGE + 1) * PLANE] = grad_ref[lev]

            def fill(p_ref, at):
                for n in range(CHUNK):
                    store = storing(p_ref, c, n * PLANE)
                    build_inner(store, act_ref, src_ref, None, 0, lev, at * CHUNK + n)

            def gather(p_ref, at):
                starts = [(at * CHUNK + 2 - dx) * PLANE for dx in range(3)]
                out_ref[...] += lax.dot_general(
                    jnp.concatenate([g_ref[:, i : i + wide] for i in starts], axis=0),
                    p_ref[...],
                    (((1,), (1,)), ((), ())),
                    preferred_element_type=f32,
                )

            fill(bufs[0], 0)
            for at in range(chunks):
                if at + 1 < chunks:
                    fill(bufs[(at + 1) % 2], at + 1)
                gather(bufs[at % 2], at)

        return 0

    lax.fori_loop(0, 2, level, 0)


def wgrad(active, src, grads, depth):
    levels, c, vox = src.shape
    whole = pl.BlockSpec(memory_space=pltpu.VMEM)
    return pl.pallas_call(
        wgrad_kernel,
        in_specs=[pl.BlockSpec(memory_space=pltpu.SMEM)] + [whole] * 2,
        out_specs=whole,
        out_shape=jax.ShapeDtypeStruct((3 * c, depth), f32),
        scratch_shapes=[
            pltpu.VMEM((depth, CHUNK * PLANE), bf16),
            pltpu.VMEM((depth, CHUNK * PLANE), bf16),
            pltpu.VMEM((c, (EDGE + 2) * PLANE), bf16),
        ],
        name="wgrad",
    )(active, src, grads)


def rim_kernel(
    sum_ref, gxl_ref, gxh_ref, gyl_ref, gyh_ref, xw_ref, xe_ref, ys_ref, yn_ref,
    out_ref, px_ref, py_ref,
):
    c = gxl_ref.shape[2]
    levels = gxl_ref.shape[1]
    px_ref[:, NEAR * c :] = jnp.zeros_like(px_ref[:, NEAR * c :])
    py_ref[...] = jnp.zeros_like(py_ref)

    def both(ref):
        return jnp.concatenate([ref[1, k] for k in range(levels)], axis=1)

    def gathered(left, right):
        return lax.dot_general(left, right, (((1,), (1,)), ((), ())), preferred_element_type=f32)

    for side, halo in enumerate((xw_ref, xe_ref)):
        for k in range(levels):
            build_outer(storing(px_ref.at[side], c, k * PLANE), halo[0, k])
    for side, halo in enumerate((ys_ref, yn_ref)):
        for k in range(levels):

            def store(at, half, value):
                row = 64 * side + (at % 3) * c
                col = k * PLANE + half * 128
                py_ref[side, at // 3, row : row + c, col : col + 128] = value

            build_outer(store, halo[0, k])
    split = py_ref.shape[2]
    far = out_ref.shape[1] - split
    for dx in range(3):
        rows = slice(dx * c, (dx + 1) * c)
        total = sum_ref[rows]
        if dx != 1:
            own = gxl_ref if dx == 0 else gxh_ref
            total = total + gathered(both(own), px_ref[dx // 2])
        low = total[:, :split] + gathered(both(gyl_ref), py_ref[0, dx])
        high = total[:, far:] + gathered(both(gyh_ref), py_ref[1, dx])
        out_ref[rows, :split] = low
        out_ref[rows, split:far] = total[:, split:far]
        out_ref[rows, far:] = high


def rim(sums, own, halos):
    levels, c = own[0].shape[1:3]
    depth = sums.shape[1]
    whole = pl.BlockSpec(memory_space=pltpu.VMEM)
    return pl.pallas_call(
        rim_kernel,
        in_specs=[whole] * 9,
        out_specs=whole,
        out_shape=jax.ShapeDtypeStruct(sums.shape, f32),
        scratch_shapes=[
            pltpu.VMEM((2, depth, levels * PLANE), bf16),
            pltpu.VMEM((2, 3, 384, levels * PLANE), bf16),
        ],
        name="rim",
    )(sums, *own, *halos)


def neighbours(low, high, axis):
    count = lax.axis_size(axis)
    forward = [(i, i + 1) for i in range(count - 1)]
    backward = [(j, i) for i, j in forward]
    return lax.ppermute(high, axis, forward), lax.ppermute(low, axis, backward)


def body(features, grad_out, weight, active):
    levels, c, vox = features.shape[2:]
    depth = -(-NEAR * c // 128) * 128
    fields = features.reshape(levels, c, vox)
    grads = grad_out.reshape(levels, c, vox)
    own = pack(active, fields, grads)
    halos = neighbours(own[0], own[1], "gx") + neighbours(own[2], own[3], "gy")

    cube = weight.reshape(c, 3, NEAR, c)
    ahead = cube.transpose(1, 0, 2, 3)
    back = cube[:, ::-1, ::-1].transpose(1, 3, 2, 0)
    both = jnp.stack([ahead, back]).reshape(2, 3 * c, NEAR * c)
    both = jnp.pad(both, ((0, 0), (0, 0), (0, depth - NEAR * c)))

    gw = rim(wgrad(active, fields, grads, depth), own, halos)
    parts = lax.axis_size("gx") * lax.axis_size("gy")
    flat = gw[:, : NEAR * c].reshape(3, c, NEAR * c).transpose(1, 0, 2).reshape(parts, -1)
    share = flat.shape[1]
    rows = -(-share // 1024) * 8
    flat = jnp.pad(flat, ((0, 0), (0, rows * 128 - share))).reshape(parts, rows, 128)
    swapped = lax.all_to_all(flat, ("gx", "gy"), 0, 0, tiled=True)
    norm_scale = 1.0 / math.sqrt(parts * levels * vox)
    summed = swapped.sum(0).reshape(-1)[:share] * norm_scale

    out, grad_in = conv(active, fields, grads, halos, both)
    return out[None, None], grad_in[None, None], summed


def solution(mesh):
    placed = (
        P("gx", "gy", None, None, None),
        P("gx", "gy", None, None, None),
        P(),
        P("gx", "gy", None),
    )
    return jax.shard_map(
        body,
        mesh=mesh,
        in_specs=placed,
        out_specs=(
            P("gx", "gy", None, None, None),
            P("gx", "gy", None, None, None),
            P(("gx", "gy")),
        ),
        check_vma=False,
    )
```

time: 82.7 us -> 74.6 us (0.902)
  the two profiles are of different devices: /device:TPU:1 before, /device:TPU:15 now
where the time goes in v3:
time: 74.6 us; the launch traced here: 74 us
  Pallas kernels  40.4 us (54%)
  starting transfers between devices  21.9 us (29%)
  local copies, waits for them, and re-layouts  9.12 us (12%)
  other arithmetic  1.87 us (3%)
  between operations  0.8 us (1%)
    pallas_call x1, Pallas kernels, conv(): pl.pallas_call(conv_kernel, in_specs=[pl.BlockSpec(memory_space=pltpu.SME...  22 us
    pallas_call x1, Pallas kernels, wgrad(): pl.pallas_call(wgrad_kernel, in_specs=[pl.BlockSpec(memory_space=pltpu.SM...  10.5 us
    all_to_all x1, starting transfers between devices, body(): swapped = lax.all_to_all(flat, ('gx', 'gy'), 0, 0, tiled=True)  9.91 us
    ppermute x2, starting transfers between devices, neighbours(): lax.ppermute(low, axis, backward)  7.14 us
    ppermute x2, starting transfers between devices, neighbours(): lax.ppermute(high, axis, forward)  4.83 us
    pallas_call x1, Pallas kernels, rim(): pl.pallas_call(rim_kernel, in_specs=[whole] * 9, out_specs=whole, out_sha...  4.75 us
    pallas_call x1, Pallas kernels, pack(): pl.pallas_call(pack_kernel, grid=(levels,), in_specs=[pl.BlockSpec(memory...  3.11 us
    reshape x2, local copies, waits for them, and re-layouts, body(): gw[:, :NEAR * c].reshape(3, c, NEAR * c).transpose(1, 0, 2)  3.07 us
  transfers between devices with their start and end apart: 5, of which 0 were waited for; matrix products, arithmetic and copies ran while one was open for 6% of the time, Pallas kernels for 44%

profile of v3, /device:TPU:15, one launch (start us, length us, event | category | flops | bytes accessed | tf_op | source)
XLA Modules:
  0.0 74.0 jit_solution(8221645348175663839)
XLA Ops:
  0.6 3.1 %pack_faces.1 = (bf16[2,2,96,256]{3,2,1,0:T(8,128)(2,1)}, bf16[2,2,96,256]{3,2,1,0:T(8,128)(2,1)}, bf16[2,2,96,256]{3,2,1,0:T(8,128)(2,1)}, bf16[2,2,96,256]{3,2,1,0:T(8,128)(2,1)}) custom-call(s32[1,1,2]{2,1,0:T(1,128)} %act_ref.5, bf16[2,96,4096]{2,1,0:T(8,128)(2,1)} %bitcast.18, bf16[2,96,4096]{2,1,0:T(8,128)(2,1)} %bitcast.21), custom_call_target="tpu_custom_call" | custom-call | tf_op jit(solution)/shard_map/pack_faces/pallas_call | solution.py:57
  3.7 1.3 %collective-permute-start = (bf16[2,2,96,256]{3,2,1,0:T(8,128)(2,1)}, bf16[2,2,96,256]{3,2,1,0:T(8,128)(2,1)S(1)}, u32[]{:S(2)}, u32[]{:S(2)}) collective-permute-start(bf16[2,2,96,256]{3,2,1,0:T(8,128)(2,1)} %get-tuple-element.9.gxh_ref), channel_id=1, source_target_pairs={{0,16},{16,32},{32,48},{48,64},{64,80},{80,96},{96,112},{1,17},{17... | collective-permute-start | bytes 589832 | tf_op jit(solution)/shard_map/ppermute | solution.py:362
  5.0 3.2 %collective-permute-start.1 = (bf16[2,2,96,256]{3,2,1,0:T(8,128)(2,1)}, bf16[2,2,96,256]{3,2,1,0:T(8,128)(2,1)S(1)}, u32[]{:S(2)}, u32[]{:S(2)}) collective-permute-start(bf16[2,2,96,256]{3,2,1,0:T(8,128)(2,1)} %get-tuple-element.10.gxl_ref), channel_id=1, source_target_pairs={{16,0},{32,16},{48,32},{64,48},{80,64},{96,80},{112,96},{17,1},{33... | collective-permute-start | bytes 589832 | tf_op jit(solution)/shard_map/ppermute | solution.py:362
  8.2 3.5 %collective-permute-start.2 = (bf16[2,2,96,256]{3,2,1,0:T(8,128)(2,1)}, bf16[2,2,96,256]{3,2,1,0:T(8,128)(2,1)S(1)}, u32[]{:S(2)}, u32[]{:S(2)}) collective-permute-start(bf16[2,2,96,256]{3,2,1,0:T(8,128)(2,1)} %get-tuple-element.11.gyh_ref), channel_id=1, source_target_pairs={{0,1},{1,2},{2,3},{3,4},{4,5},{5,6},{6,7},{7,8},{8,9},{9,10},{10,1... | collective-permute-start | bytes 589832 | tf_op jit(solution)/shard_map/ppermute | solution.py:362
  11.8 3.9 %collective-permute-start.3 = (bf16[2,2,96,256]{3,2,1,0:T(8,128)(2,1)}, bf16[2,2,96,256]{3,2,1,0:T(8,128)(2,1)S(1)}, u32[]{:S(2)}, u32[]{:S(2)}) collective-permute-start(bf16[2,2,96,256]{3,2,1,0:T(8,128)(2,1)} %get-tuple-element.12.gyl_ref), channel_id=1, source_target_pairs={{1,0},{2,1},{3,2},{4,3},{5,4},{6,5},{7,6},{8,7},{9,8},{10,9},{11,1... | collective-permute-start | bytes 589832 | tf_op jit(solution)/shard_map/ppermute | solution.py:362
  15.7 10.5 %wgrad.1.sum_ref = f32[288,896]{1,0:T(8,128)} custom-call(s32[1,1,2]{2,1,0:T(1,128)} %act_ref.5, bf16[2,96,4096]{2,1,0:T(8,128)(2,1)} %bitcast.19, bf16[2,96,4096]{2,1,0:T(8,128)(2,1)} %bitcast.22), custom_call_target="tpu_custom_call" | custom-call | tf_op jit(solution)/shard_map/wgrad/pallas_call | solution.py:285
  26.3 0.6 copy-done
  26.9 0.1 copy-done.1
  27.1 0.7 copy-done.3
  27.7 4.8 %rim.1 = f32[288,896]{1,0:T(8,128)} custom-call(f32[288,896]{1,0:T(8,128)} %wgrad.1.sum_ref, bf16[2,2,96,256]{3,2,1,0:T(8,128)(2,1)} %get-tuple-element.10.gxl_ref, bf16[2,2,96,256]{3,2,1,0:T(8,128)(2,1)} %get-tuple-element.9.gxh_ref, bf16[2,2,96,256]{3,2,1,0:T(8,128)(2,1)} %get-tuple-element.12.gyl_ref, bf16[2,2,96,256]{3,2,1,0:T(8,128)(2,1)} %get-tuple-element.11.gyh_ref, ...), custom_call_target="tpu_custom_call" | custom-call | tf_op jit(solution)/shard_map/rim/pallas_call | solution.py:345
  32.5 1.9 %copy.21 = f32[3,96,864]{2,0,1:T(4,128)S(1)} copy(f32[3,96,864]{2,1,0:T(8,128)} %bitcast.27) | data formatting | bytes 1990656 | tf_op jit(solution)/shard_map/reshape | solution.py:381
  34.4 1.1 %reshape.36 = f32[128,1944]{1,0:T(8,128)S(1)} reshape(f32[96,3,864]{2,1,0:T(4,128)S(1)} %bitcast.26) | data formatting | bytes 1990656 | tf_op jit(solution)/shard_map/reshape | solution.py:381
  35.6 0.1 pad_bitcast_fusion
  35.6 1.2 %copy.19 = f32[16,8,16,128]{3,2,1,0:T(8,128)} copy(f32[16,8,16,128]{3,1,2,0:T(8,128)S(1)} %pad_bitcast_fusion) | data formatting | bytes 2097152
  36.8 9.9 %all-to-all-start = ((f32[128,16,128]{2,1,0:T(8,128)}), f32[128,16,128]{2,1,0:T(8,128)S(1)}, u32[]{:S(2)}, u32[]{:S(2)}) async-start(f32[128,16,128]{2,1,0:T(8,128)} %bitcast.12), calls=%async_computation | async-start | bytes 2097152 | tf_op jit(solution)/shard_map/all_to_all | solution.py:385
  46.7 0.3 copy.9
  47.1 0.3 copy.16
  47.5 0.8 %reshape.40 = bf16[1,288,864]{2,1,0:T(8,128)(2,1)S(1)} reshape(bf16[3,96,9,96]{3,2,1,0:T(8,128)(2,1)S(1)} %copy.16) | data formatting | bytes 995328 | tf_op jit(solution)/shard_map/stack | solution.py:376
  48.3 1.1 %copy.15 = bf16[3,96,9,96]{3,2,1,0:T(8,128)(2,1)S(1)} copy(bf16[3,96,9,96]{1,3,2,0:T(8,128)(2,1)S(1)} %bitcast.25) | data formatting | bytes 995328 | tf_op jit(solution)/shard_map/stack | solution.py:376
  49.4 0.8 %reshape.39 = bf16[1,288,864]{2,1,0:T(8,128)(2,1)S(1)} reshape(bf16[3,96,9,96]{3,2,1,0:T(8,128)(2,1)S(1)} %copy.15) | data formatting | bytes 995328 | tf_op jit(solution)/shard_map/stack | solution.py:376
  50.1 1.1 %fusion.2.w_ref = bf16[2,288,896]{2,1,0:T(8,128)(2,1)} fusion(bf16[1,288,864]{2,1,0:T(8,128)(2,1)S(1)} %reshape.40, bf16[1,288,864]{2,1,0:T(8,128)(2,1)S(1)} %reshape.39), kind=kLoop, calls=%fused_computation.5 | loop fusion | flops 3612672 | bytes 2027520 | tf_op jit(solution)/shard_map/stack | solution.py:376
  51.3 22.0 %conv.1 = (bf16[2,96,4096]{2,1,0:T(8,128)(2,1)}, bf16[2,96,4096]{2,1,0:T(8,128)(2,1)}) custom-call(s32[1,1,2]{2,1,0:T(1,128)} %act_ref.5, bf16[2,96,4096]{2,1,0:T(8,128)(2,1)} %bitcast.20, bf16[2,96,4096]{2,1,0:T(8,128)(2,1)} %bitcast.23, bf16[2,2,96,256]{3,2,1,0:T(8,128)(2,1)} %copy-done, bf16[2,2,96,256]{3,2,1,0:T(8,128)(2,1)} %copy-done.1, ...), custom_call_target="tpu_custom_call" | custom-call | tf_op jit(solution)/shard_map/conv/pallas_call | solution.py:223
  73.3 0.1 reduce_sum.9
  73.4 0.6 slice_multiply_fusion
  (13 shorter events, 0.1 us)
Async XLA Ops:
  3.7 22.5 %collective-permute-start = (bf16[2,2,96,256]{3,2,1,0:T(8,128)(2,1)}, bf16[2,2,96,256]{3,2,1,0:T(8,128)(2,1)S(1)}, u32[]{:S(2)}, u32[]{:S(2)}) collective-permute-start(bf16[2,2,96,256]{3,2,1,0:T(8,128)(2,1)} %get-tuple-element.9.gxh_ref), channel_id=1, source_target_pairs={{0,16},{16,32},{32,48},{48,64},{64,80},{80,96},{96,112},{1,17},{17... | collective-permute-start | bytes 589832 | tf_op jit(solution)/shard_map/ppermute | solution.py:362
  5.0 21.2 %collective-permute-start.1 = (bf16[2,2,96,256]{3,2,1,0:T(8,128)(2,1)}, bf16[2,2,96,256]{3,2,1,0:T(8,128)(2,1)S(1)}, u32[]{:S(2)}, u32[]{:S(2)}) collective-permute-start(bf16[2,2,96,256]{3,2,1,0:T(8,128)(2,1)} %get-tuple-element.10.gxl_ref), channel_id=1, source_target_pairs={{16,0},{32,16},{48,32},{64,48},{80,64},{96,80},{112,96},{17,1},{33... | collective-permute-start | bytes 589832 | tf_op jit(solution)/shard_map/ppermute | solution.py:362
  8.2 18.0 %collective-permute-start.2 = (bf16[2,2,96,256]{3,2,1,0:T(8,128)(2,1)}, bf16[2,2,96,256]{3,2,1,0:T(8,128)(2,1)S(1)}, u32[]{:S(2)}, u32[]{:S(2)}) collective-permute-start(bf16[2,2,96,256]{3,2,1,0:T(8,128)(2,1)} %get-tuple-element.11.gyh_ref), channel_id=1, source_target_pairs={{0,1},{1,2},{2,3},{3,4},{4,5},{5,6},{6,7},{7,8},{8,9},{9,10},{10,1... | collective-permute-start | bytes 589832 | tf_op jit(solution)/shard_map/ppermute | solution.py:362
  11.8 14.5 %collective-permute-start.3 = (bf16[2,2,96,256]{3,2,1,0:T(8,128)(2,1)}, bf16[2,2,96,256]{3,2,1,0:T(8,128)(2,1)S(1)}, u32[]{:S(2)}, u32[]{:S(2)}) collective-permute-start(bf16[2,2,96,256]{3,2,1,0:T(8,128)(2,1)} %get-tuple-element.12.gyl_ref), channel_id=1, source_target_pairs={{1,0},{2,1},{3,2},{4,3},{5,4},{6,5},{7,6},{8,7},{9,8},{10,9},{11,1... | collective-permute-start | bytes 589832 | tf_op jit(solution)/shard_map/ppermute | solution.py:362
  26.2 0.7 copy-start
  26.2 0.7 %copy-start.1 = (bf16[2,2,96,256]{3,2,1,0:T(8,128)(2,1)}, bf16[2,2,96,256]{3,2,1,0:T(8,128)(2,1)S(1)}, u32[]{:S(2)}) copy-start(bf16[2,2,96,256]{3,2,1,0:T(8,128)(2,1)S(1)} %collective-permute-done.1.xe_ref) | copy-start | bytes 589828
  26.3 0.8 %copy-start.2 = (bf16[2,2,96,256]{3,2,1,0:T(8,128)(2,1)}, bf16[2,2,96,256]{3,2,1,0:T(8,128)(2,1)S(1)}, u32[]{:S(2)}) copy-start(bf16[2,2,96,256]{3,2,1,0:T(8,128)(2,1)S(1)} %collective-permute-done.2.ys_ref) | copy-start | bytes 589828
  27.1 0.7 copy-start.3
  36.8 9.9 %copy-start.4 = (bf16[96,2592]{1,0:T(8,128)(2,1)S(1)}, bf16[96,2592]{1,0:T(8,128)(2,1)}, u32[]{:S(2)}) copy-start(bf16[96,2592]{1,0:T(8,128)(2,1)} %param.6) | copy-start | bytes 1492996
  36.8 36.5 %all-to-all-start = ((f32[128,16,128]{2,1,0:T(8,128)}), f32[128,16,128]{2,1,0:T(8,128)S(1)}, u32[]{:S(2)}, u32[]{:S(2)}) async-start(f32[128,16,128]{2,1,0:T(8,128)} %bitcast.12), calls=%async_computation | async-start | bytes 2097152 | tf_op jit(solution)/shard_map/all_to_all | solution.py:385

commit v4 on v3

--- a/solution.py
+++ b/solution.py
@@ -10,6 +10,7 @@
 
 EDGE = 16
 CONV_CHUNK = 3
+GRANT = 20 << 20
 CHUNK = 4
 PLANE = EDGE * EDGE
 NEAR = 9
@@ -25,43 +26,107 @@
     return jnp.where(mask, a, b)
 
 
-def pack_kernel(act_ref, f_ref, g_ref, xlo_ref, xhi_ref, ylo_ref, yhi_ref):
-    c = f_ref.shape[0]
-    live = act_ref[0, 0, pl.program_id(0)].astype(f32).astype(bf16)
+def spread_weight(weight_ref, w_ref, wide_ref, turn_ref):
+    c, count = weight_ref.shape
+    depth = w_ref.shape[2]
+    wide_ref[:, wide_ref.shape[1] - 128 :] = jnp.zeros((c, 128), bf16)
+    wide_ref[:, :count] = weight_ref[...]
+    inside = lanes_of((c, depth)) < NEAR * c
+    lane = lanes_of((c, 128))
+    eye = (lane == lax.broadcasted_iota(jnp.int32, (c, 128), 0)).astype(f32).astype(bf16)
+    for dx in range(3):
+        start = dx * NEAR * c
+        tile = start // 128 * 128
+        value = wide_ref[:, tile : tile + (depth if dx == 0 else depth + 128)]
+        if dx:
+            value = pltpu.roll(value, depth + 128 - (start - tile), 1)[:, :depth]
+        w_ref[0, dx * c : (dx + 1) * c] = pick(inside, value, jnp.zeros((c, depth), bf16))
+        for near in range(NEAR):
+            start = (3 * NEAR - 1 - dx * NEAR - near) * c
+            tile, off = start // 128 * 128, start % 128
+            value = turned(wide_ref[:, tile : tile + 128], -off)
+            if off + c > 128:
+                after = turned(wide_ref[:, tile + 128 : tile + 256], -off)
+                value = pick(lane < 128 - off, value, after)
+            turn_ref[dx, near * c : (near + 1) * c] = value
+        turn_ref[dx, NEAR * c :] = jnp.zeros((depth - NEAR * c, 128), bf16)
+        swapped = lax.dot_general(
+            eye, turn_ref[dx], (((1,), (1,)), ((), ())), preferred_element_type=f32
+        )
+        w_ref[1, dx * c : (dx + 1) * c] = swapped.astype(bf16)
+
+
+def pack_kernel(
+    act_ref, f_ref, g_ref, weight_ref, xlo_ref, xhi_ref, ylo_ref, yhi_ref, both_ref, w_far,
+    w_ref, raw_ref, wide_ref, turn_ref, raw_sem, sem,
+):
+    levels, c, _ = f_ref.shape
     half = lanes_of((c, 128)) // EDGE
-    for arr, src in enumerate((f_ref, g_ref)):
-        xlo_ref[arr] = src[:, 0:PLANE] * live
-        xhi_ref[arr] = src[:, 15 * PLANE : 16 * PLANE] * live
+    raw = pltpu.make_async_copy(weight_ref, raw_ref, raw_sem)
+    raw.start()
+    loads = {}
+    for lev in range(levels):
+        for arr, ref in enumerate((f_ref, g_ref)):
+            load = pltpu.make_async_copy(ref.at[lev], both_ref.at[arr, lev], sem.at[arr, lev])
+            load.start()
+            loads[arr, lev] = load
+    raw.wait()
+    spread_weight(raw_ref, w_ref, wide_ref, turn_ref)
+    spread = pltpu.make_async_copy(w_ref, w_far, raw_sem)
+    spread.start()
+    for (arr, lev), load in loads.items():
+        load.wait()
+        src = both_ref.at[arr]
+        live = act_ref[0, 0, lev].astype(f32).astype(bf16)
+        xlo_ref[arr, lev] = src[lev, :, 0:PLANE] * live
+        xhi_ref[arr, lev] = src[lev, :, 15 * PLANE : 16 * PLANE] * live
         for h in range(2):
             low = jnp.zeros((c, 128), bf16)
             high = jnp.zeros((c, 128), bf16)
             for xs in range(8):
-                x = 8 * h + xs
-                a = src[:, x * PLANE : x * PLANE + 128]
-                b = src[:, x * PLANE + 128 : x * PLANE + 256]
-                if xs:
-                    a = pltpu.roll(a, 16 * xs, 1)
-                if xs != 7:
-                    b = pltpu.roll(b, 16 * xs + 16, 1)
+                at = (8 * h + xs) * PLANE
+                a = turned(src[lev, :, at : at + 128], EDGE * xs)
+                b = turned(src[lev, :, at + 128 : at + 256], EDGE * xs + EDGE)
                 low = pick(half == xs, a, low)
                 high = pick(half == xs, b, high)
-            ylo_ref[arr, :, h * 128 : h * 128 + 128] = low * live
-            yhi_ref[arr, :, h * 128 : h * 128 + 128] = high * live
-
-
-def pack(active, features, grads):
+            ylo_ref[arr, lev, :, h * 128 : h * 128 + 128] = low * live
+            yhi_ref[arr, lev, :, h * 128 : h * 128 + 128] = high * live
+    spread.wait()
+
+
+def near(shape, dtype):
+    return pltpu.VMEM(shape, dtype)
+
+
+def held(*arrays):
+    return [pltpu.with_memory_space_constraint(a, pltpu.VMEM) for a in arrays]
+
+
+def far_off(*arrays):
+    return [pltpu.with_memory_space_constraint(a, pltpu.HBM) for a in arrays]
+
+
+def pack(active, features, grads, weight, depth):
     levels, c, vox = features.shape
-    face = jax.ShapeDtypeStruct((2, levels, c, PLANE), bf16)
-    brick = pl.BlockSpec((None, c, vox), lambda k: (k, 0, 0))
-    side = pl.BlockSpec((2, None, c, PLANE), lambda k: (0, k, 0, 0))
+    apart = pl.BlockSpec(memory_space=pltpu.HBM)
+    whole = pl.BlockSpec(memory_space=pltpu.VMEM)
     return pl.pallas_call(
         pack_kernel,
-        grid=(levels,),
-        in_specs=[pl.BlockSpec(memory_space=pltpu.SMEM), brick, brick],
-        out_specs=[side] * 4,
-        out_shape=[face] * 4,
+        in_specs=[pl.BlockSpec(memory_space=pltpu.SMEM)] + [apart] * 3,
+        out_specs=[whole] * 5 + [apart],
+        out_shape=[near((2, levels, c, PLANE), bf16)] * 4 + [near((2, levels, c, vox), bf16)]
+        + [pltpu.HBM((2, 3 * c, depth), bf16)],
+        scratch_shapes=[
+            pltpu.VMEM((2, 3 * c, depth), bf16),
+            pltpu.VMEM(weight.shape, bf16),
+            pltpu.VMEM((c, -(-weight.shape[1] // 128) * 128), bf16),
+            pltpu.VMEM((3, depth, 128), bf16),
+            pltpu.SemaphoreType.DMA,
+            pltpu.SemaphoreType.DMA((2, levels)),
+        ],
         name="pack_faces",
-    )(active, features, grads)
+        compiler_params=pltpu.CompilerParams(vmem_limit_bytes=GRANT),
+    )(active, *far_off(features, grads, weight))
 
 
 def turned(value, amount):
@@ -134,14 +199,22 @@
 
 
 def conv_kernel(
-    act_ref, f_ref, g_ref, xw_ref, xe_ref, ys_ref, yn_ref, w_ref, out_ref, back_ref,
-    src_ref, pa_ref, pb_ref, acc_ref, res_ref, in_sem, out_sem,
+    act_ref, src_ref, xw_far, xe_far, ys_far, yn_far, w_far, out_ref, back_ref,
+    xw_ref, xe_ref, ys_ref, yn_ref, w_ref, pa_ref, pb_ref, acc_ref, res_ref, in_sem, out_sem,
 ):
-    c = src_ref.shape[2]
-    levels = src_ref.shape[1]
+    _, levels, c, _ = src_ref.shape
     chunks = (EDGE + 2) // CONV_CHUNK
-    loads = [pltpu.make_async_copy(r, src_ref.at[i], in_sem.at[i]) for i, r in enumerate((f_ref, g_ref))]
-    for load in loads:
+    pairs = (
+        (ys_far, ys_ref), (yn_far, yn_ref), (xw_far, xw_ref), (w_far, w_ref), (xe_far, xe_ref)
+    )
+    loads = [
+        [
+            pltpu.make_async_copy(far.at[arr], to.at[arr], in_sem.at[arr, i])
+            for i, (far, to) in enumerate(pairs)
+        ]
+        for arr in range(2)
+    ]
+    for load in loads[0] + loads[1]:
         load.start()
     bufs = (pa_ref, pb_ref)
     for p_ref in bufs:
@@ -160,11 +233,12 @@
         arr, lev = item // levels, lax.rem(item, levels)
         slot = lax.rem(lev, 2)
 
-        for i, load in enumerate(loads):
+        for i in range(2):
 
             @pl.when(item == i * levels)
             def _():
-                load.wait()
+                for load in loads[i]:
+                    load.wait()
 
         @pl.when(item >= 2)
         def _():
@@ -215,30 +289,34 @@
         save(1, lev, False)
 
 
-def conv(active, fields, grads, faces, weights):
-    levels, c, vox = fields.shape
+def conv(active, fields, faces, weights):
+    _, levels, c, vox = fields.shape
     depth = weights.shape[2]
     whole = pl.BlockSpec(memory_space=pltpu.VMEM)
-    apart = pl.BlockSpec(memory_space=pl.ANY)
+    apart = pl.BlockSpec(memory_space=pltpu.HBM)
+    side = pltpu.VMEM((2, levels, c, PLANE), bf16)
     return pl.pallas_call(
         conv_kernel,
-        in_specs=[pl.BlockSpec(memory_space=pltpu.SMEM)] + [apart] * 2 + [whole] * 5,
+        in_specs=[pl.BlockSpec(memory_space=pltpu.SMEM), whole] + [apart] * 5,
         out_specs=[apart] * 2,
         out_shape=[jax.ShapeDtypeStruct((levels, c, vox), bf16)] * 2,
-        scratch_shapes=[
-            pltpu.VMEM((2, levels, c, vox), bf16),
+        scratch_shapes=[side] * 4
+        + [
+            pltpu.VMEM((2, 3 * c, depth), bf16),
             pltpu.VMEM((depth, CONV_CHUNK * PLANE), bf16),
             pltpu.VMEM((depth, CONV_CHUNK * PLANE), bf16),
             pltpu.VMEM((2, c, PLANE), f32),
             pltpu.VMEM((2, c, vox), bf16),
-            pltpu.SemaphoreType.DMA((2,)),
+            pltpu.SemaphoreType.DMA((2, 5)),
             pltpu.SemaphoreType.DMA((2,)),
         ],
         name="conv",
-    )(active, fields, grads, *faces, weights)
-
-
-def wgrad_kernel(act_ref, src_ref, grad_ref, out_ref, pa_ref, pb_ref, g_ref):
+        compiler_params=pltpu.CompilerParams(vmem_limit_bytes=GRANT),
+    )(active, *held(fields), *far_off(*faces, weights))
+
+
+def wgrad_kernel(act_ref, both_ref, out_ref, pa_ref, pb_ref, g_ref):
+    src_ref, grad_ref = both_ref.at[0], both_ref.at[1]
     c = src_ref.shape[1]
     chunks = EDGE // CHUNK
     wide = CHUNK * PLANE
@@ -279,26 +357,27 @@
     lax.fori_loop(0, 2, level, 0)
 
 
-def wgrad(active, src, grads, depth):
-    levels, c, vox = src.shape
+def wgrad(active, fields, depth):
+    c = fields.shape[2]
     whole = pl.BlockSpec(memory_space=pltpu.VMEM)
     return pl.pallas_call(
         wgrad_kernel,
-        in_specs=[pl.BlockSpec(memory_space=pltpu.SMEM)] + [whole] * 2,
+        in_specs=[pl.BlockSpec(memory_space=pltpu.SMEM), whole],
         out_specs=whole,
-        out_shape=jax.ShapeDtypeStruct((3 * c, depth), f32),
+        out_shape=near((3 * c, depth), f32),
         scratch_shapes=[
             pltpu.VMEM((depth, CHUNK * PLANE), bf16),
             pltpu.VMEM((depth, CHUNK * PLANE), bf16),
             pltpu.VMEM((c, (EDGE + 2) * PLANE), bf16),
         ],
         name="wgrad",
-    )(active, src, grads)
+        compiler_params=pltpu.CompilerParams(vmem_limit_bytes=GRANT),
+    )(active, *held(fields))
 
 
 def rim_kernel(
     sum_ref, gxl_ref, gxh_ref, gyl_ref, gyh_ref, xw_ref, xe_ref, ys_ref, yn_ref,
-    out_ref, px_ref, py_ref,
+    out_far, px_ref, py_ref, row_ref, out_ref, sem,
 ):
     c = gxl_ref.shape[2]
     levels = gxl_ref.shape[1]
@@ -324,35 +403,86 @@
 
             build_outer(store, halo[0, k])
     split = py_ref.shape[2]
-    far = out_ref.shape[1] - split
+    depth = sum_ref.shape[1]
+    far = depth - split
+    end = jnp.zeros((c, 128), f32)
+    kept = None
     for dx in range(3):
-        rows = slice(dx * c, (dx + 1) * c)
-        total = sum_ref[rows]
+        total = sum_ref[dx * c : (dx + 1) * c]
         if dx != 1:
             own = gxl_ref if dx == 0 else gxh_ref
             total = total + gathered(both(own), px_ref[dx // 2])
         low = total[:, :split] + gathered(both(gyl_ref), py_ref[0, dx])
         high = total[:, far:] + gathered(both(gyh_ref), py_ref[1, dx])
-        out_ref[rows, :split] = low
-        out_ref[rows, split:far] = total[:, split:far]
-        out_ref[rows, far:] = high
-
-
-def rim(sums, own, halos):
+        total = jnp.concatenate([low, total[:, split:far], high], axis=1)
+        start = dx * NEAR * c
+        tile = start // 128 * 128
+        if dx:
+            total = pltpu.roll(jnp.concatenate([total, end], axis=1), start - tile, 1)
+            row_ref[tile // 128] = kept + total[:, :128]
+            total = total[:, 128:]
+            tile += 128
+        size = total.shape[1]
+        if dx < 2:
+            size -= 128
+            kept = total[:, size:]
+        for i in range(size // 128):
+            row_ref[tile // 128 + i] = total[:, i * 128 : i * 128 + 128]
+    scatter_rows(row_ref, out_ref, out_far, sem)
+
+
+def scatter_rows(row_ref, out_ref, out_far, sem):
+    tiles, count, _ = row_ref.shape
+    groups = count // 3
+    length = 3 * NEAR * count
+    share = 3 * length // 4
+    room = out_ref.shape[2] * 128
+    lane = lanes_of((groups, 128))
+    copies = []
+    rows = [
+        jnp.concatenate([row_ref.at[t][pl.ds(r, groups, stride=3), :] for t in range(tiles)], axis=1)
+        for r in range(3)
+    ]
+    for q in range(4):
+        first = q * share
+        r, start = first // length, first % length
+        tile = start // 128 * 128
+        value = rows[r][:, tile : tile + room]
+        if start - tile:
+            value = pltpu.roll(value, value.shape[1] - (start - tile), 1)
+        left = length - start
+        if left < share:
+            seam = left // 128 * 128
+            after = rows[r + 1][:, : room - seam]
+            after = pltpu.roll(after, left - seam, 1)
+            middle = pick(lane < left - seam, value[:, seam : seam + 128], after[:, :128])
+            value = jnp.concatenate([value[:, :seam], middle, after[:, 128:]], axis=1)
+        out_ref[q] = value.reshape(groups, room // 128, 128)
+        copies.append(pltpu.make_async_copy(out_ref.at[q], out_far.at[:, q], sem.at[q]))
+        copies[-1].start()
+    for copy in copies:
+        copy.wait()
+
+
+def rim(sums, own, halos, rows):
     levels, c = own[0].shape[1:3]
     depth = sums.shape[1]
     whole = pl.BlockSpec(memory_space=pltpu.VMEM)
     return pl.pallas_call(
         rim_kernel,
         in_specs=[whole] * 9,
-        out_specs=whole,
-        out_shape=jax.ShapeDtypeStruct(sums.shape, f32),
+        out_specs=pl.BlockSpec(memory_space=pltpu.HBM),
+        out_shape=pltpu.HBM((c // 3, 4, rows, 128), f32),
         scratch_shapes=[
             pltpu.VMEM((2, depth, levels * PLANE), bf16),
             pltpu.VMEM((2, 3, 384, levels * PLANE), bf16),
+            pltpu.VMEM((-(-3 * NEAR * c // 128), c, 128), f32),
+            pltpu.VMEM((4, c // 3, rows, 128), f32),
+            pltpu.SemaphoreType.DMA((4,)),
         ],
         name="rim",
-    )(sums, *own, *halos)
+        compiler_params=pltpu.CompilerParams(vmem_limit_bytes=GRANT),
+    )(*held(sums, *own, *halos))
 
 
 def neighbours(low, high, axis):
@@ -364,29 +494,26 @@
 
 def body(features, grad_out, weight, active):
     levels, c, vox = features.shape[2:]
+    active, = far_off(active)
     depth = -(-NEAR * c // 128) * 128
     fields = features.reshape(levels, c, vox)
     grads = grad_out.reshape(levels, c, vox)
-    own = pack(active, fields, grads)
+    *own, cells, weights = pack(active, fields, grads, weight, depth)
     halos = neighbours(own[0], own[1], "gx") + neighbours(own[2], own[3], "gy")
 
-    cube = weight.reshape(c, 3, NEAR, c)
-    ahead = cube.transpose(1, 0, 2, 3)
-    back = cube[:, ::-1, ::-1].transpose(1, 3, 2, 0)
-    both = jnp.stack([ahead, back]).reshape(2, 3 * c, NEAR * c)
-    both = jnp.pad(both, ((0, 0), (0, 0), (0, depth - NEAR * c)))
-
-    gw = rim(wgrad(active, fields, grads, depth), own, halos)
+    unit = 3 * 3 * NEAR * c // 4
+    rows = -(-unit // 1024) * 8
+    shares = rim(wgrad(active, cells, depth), own, halos, rows).reshape(-1, rows, 128)
     parts = lax.axis_size("gx") * lax.axis_size("gy")
-    flat = gw[:, : NEAR * c].reshape(3, c, NEAR * c).transpose(1, 0, 2).reshape(parts, -1)
-    share = flat.shape[1]
-    rows = -(-share // 1024) * 8
-    flat = jnp.pad(flat, ((0, 0), (0, rows * 128 - share))).reshape(parts, rows, 128)
-    swapped = lax.all_to_all(flat, ("gx", "gy"), 0, 0, tiled=True)
+    share = weight.size // parts
+    if parts != shares.shape[0]:
+        shares = shares.reshape(-1, rows * 128)[:, :unit].reshape(parts, share)
+        shares = jnp.pad(shares, ((0, 0), (0, -share % 1024))).reshape(parts, -1, 128)
+    swapped = lax.all_to_all(shares, ("gx", "gy"), 0, 0, tiled=True)
     norm_scale = 1.0 / math.sqrt(parts * levels * vox)
     summed = swapped.sum(0).reshape(-1)[:share] * norm_scale
 
-    out, grad_in = conv(active, fields, grads, halos, both)
+    out, grad_in = conv(active, cells, halos, weights)
     return out[None, None], grad_in[None, None], summed
 
 

time: 74.6 us -> 62.7 us (0.84)
  the two profiles are of different devices: /device:TPU:15 before, /device:TPU:1 now
where the time goes in v4:
time: 62.7 us; the launch traced here: 62.8 us
  Pallas kernels  36.6 us (58%)
  starting transfers between devices  23.4 us (37%)
  other arithmetic  1.97 us (3%)
  between operations  0.81 us (1%)
    pallas_call x1, Pallas kernels, conv(): pl.pallas_call(conv_kernel, in_specs=[pl.BlockSpec(memory_space=pltpu.SME...  20.9 us
    all_to_all x1, starting transfers between devices, body(): swapped = lax.all_to_all(shares, ('gx', 'gy'), 0, 0, tiled=True)  12.1 us
    pallas_call x1, Pallas kernels, wgrad(): pl.pallas_call(wgrad_kernel, in_specs=[pl.BlockSpec(memory_space=pltpu.SM...  8.31 us
    ppermute x2, starting transfers between devices, neighbours(): lax.ppermute(high, axis, forward)  8.05 us
    pallas_call x1, Pallas kernels, pack(): pl.pallas_call(pack_kernel, in_specs=[pl.BlockSpec(memory_space=pltpu.SME...  4.04 us
    pallas_call x1, Pallas kernels, rim(): pl.pallas_call(rim_kernel, in_specs=[whole] * 9, out_specs=pl.BlockSpec(m...  3.38 us
    ppermute x2, starting transfers between devices, neighbours(): lax.ppermute(low, axis, backward)  3.21 us
    reduce_sum x1, other arithmetic, body(): summed = swapped.sum(0).reshape(-1)[:share] * norm_scale  1.36 us
  transfers between devices with their start and end apart: 5, of which 0 were waited for; matrix products, arithmetic and copies ran while one was open for 0% of the time, Pallas kernels for 47%

profile of v4, /device:TPU:1, one launch (start us, length us, event | category | flops | bytes accessed | tf_op | source)
XLA Modules:
  0.0 62.8 jit_solution(5126927342544773081)
XLA Ops:
  0.6 4.0 %pack_faces.1 = (bf16[2,2,96,256]{3,2,1,0:T(8,128)(2,1)S(1)}, bf16[2,2,96,256]{3,2,1,0:T(8,128)(2,1)S(1)}, bf16[2,2,96,256]{3,2,1,0:T(8,128)(2,1)S(1)}, bf16[2,2...) custom-call(s32[1,1,2]{2,1,0:T(1,128)} %act_ref.5, ...), custom_call_target="tpu_custom_call" | custom-call | tf_op jit(solution)/shard_map/pack_faces/pallas_call | solution.py:113
  4.7 4.5 %collective-permute-start = (bf16[2,2,96,256]{3,2,1,0:T(8,128)(2,1)S(1)}, bf16[2,2,96,256]{3,2,1,0:T(8,128)(2,1)S(1)}, u32[]{:S(2)}, u32[]{:S(2)}) collective-permute-start(bf16[2,2,96,256]{3,2,1,0:T(8,128)(2,1)S(1)} %get-tuple-element.12.gxh_ref), channel_id=1, source_target_pairs={{0,16},{16,32},{32,48},{48,64},{64,80},{80,96},{96,112},{1,17},{17... | collective-permute-start | bytes 589832 | tf_op jit(solution)/shard_map/ppermute | solution.py:492
  9.2 1.9 %collective-permute-start.1 = (bf16[2,2,96,256]{3,2,1,0:T(8,128)(2,1)S(1)}, bf16[2,2,96,256]{3,2,1,0:T(8,128)(2,1)S(1)}, u32[]{:S(2)}, u32[]{:S(2)}) collective-permute-start(bf16[2,2,96,256]{3,2,1,0:T(8,128)(2,1)S(1)} %get-tuple-element.13.gxl_ref), channel_id=1, source_target_pairs={{16,0},{32,16},{48,32},{64,48},{80,64},{96,80},{112,96},{17,1},{33... | collective-permute-start | bytes 589832 | tf_op jit(solution)/shard_map/ppermute | solution.py:492
  11.1 3.6 %collective-permute-start.2 = (bf16[2,2,96,256]{3,2,1,0:T(8,128)(2,1)S(1)}, bf16[2,2,96,256]{3,2,1,0:T(8,128)(2,1)S(1)}, u32[]{:S(2)}, u32[]{:S(2)}) collective-permute-start(bf16[2,2,96,256]{3,2,1,0:T(8,128)(2,1)S(1)} %get-tuple-element.14.gyh_ref), channel_id=1, source_target_pairs={{0,1},{1,2},{2,3},{3,4},{4,5},{5,6},{6,7},{7,8},{8,9},{9,10},{10,1... | collective-permute-start | bytes 589832 | tf_op jit(solution)/shard_map/ppermute | solution.py:492
  14.7 1.3 %collective-permute-start.3 = (bf16[2,2,96,256]{3,2,1,0:T(8,128)(2,1)S(1)}, bf16[2,2,96,256]{3,2,1,0:T(8,128)(2,1)S(1)}, u32[]{:S(2)}, u32[]{:S(2)}) collective-permute-start(bf16[2,2,96,256]{3,2,1,0:T(8,128)(2,1)S(1)} %get-tuple-element.15.gyl_ref), channel_id=1, source_target_pairs={{1,0},{2,1},{3,2},{4,3},{5,4},{6,5},{7,6},{8,7},{9,8},{10,9},{11,1... | collective-permute-start | bytes 589832 | tf_op jit(solution)/shard_map/ppermute | solution.py:492
  16.0 8.3 %wgrad.1.sum_ref = f32[288,896]{1,0:T(8,128)S(1)} custom-call(s32[1,1,2]{2,1,0:T(1,128)} %act_ref.5, bf16[2,2,96,4096]{3,2,1,0:T(8,128)(2,1)S(1)} %get-tuple-element.11.src_ref.both_ref), custom_call_target="tpu_custom_call" | custom-call | tf_op jit(solution)/shard_map/wgrad/pallas_call | solution.py:363
  24.3 0.0 collective-permute-done.xw_far.xw_ref
  24.3 0.0 copy-start
  24.3 0.0 collective-permute-done.1.xe_far.xe_ref
  24.3 0.0 copy-start.1
  24.3 0.0 collective-permute-done.2.ys_far.ys_ref
  24.3 0.0 copy-start.2
  24.4 0.0 collective-permute-done.3.yn_far.yn_ref
  24.4 0.0 copy-start.3
  24.4 3.4 %rim.1 = f32[32,4,16,128]{3,2,1,0:T(8,128)} custom-call(f32[288,896]{1,0:T(8,128)S(1)} %wgrad.1.sum_ref, bf16[2,2,96,256]{3,2,1,0:T(8,128)(2,1)S(1)} %get-tuple-element.13.gxl_ref, bf16[2,2,96,256]{3,2,1,0:T(8,128)(2,1)S(1)} %get-tuple-element.12.gxh_ref, bf16[2,2,96,256]{3,2,1,0:T(8,128)(2,1)S(1)} %get-tuple-element.15.gyl_ref, ...), custom_call_target="tpu_custom_call" | custom-call | tf_op jit(solution)/shard_map/rim/pallas_call | solution.py:471
  27.8 0.0 copy-done
  27.8 0.0 copy-done.1
  27.8 0.0 copy-done.2
  27.8 0.0 copy-done.3
  27.8 12.1 %all-to-all-start = ((f32[128,16,128]{2,1,0:T(8,128)}), f32[128,16,128]{2,1,0:T(8,128)}, u32[]{:S(2)}, u32[]{:S(2)}) async-start(f32[128,16,128]{2,1,0:T(8,128)} %bitcast.6), calls=%async_computation | async-start | bytes 2097152 | tf_op jit(solution)/shard_map/all_to_all | solution.py:512
  39.9 20.9 %conv.1 = (bf16[2,96,4096]{2,1,0:T(8,128)(2,1)}, bf16[2,96,4096]{2,1,0:T(8,128)(2,1)}) custom-call(s32[1,1,2]{2,1,0:T(1,128)} %act_ref.5, bf16[2,2,96,4096]{3,2,1,0:T(8,128)(2,1)S(1)} %get-tuple-element.11.src_ref.both_ref, bf16[2,2,96,256]{3,2,1,0:T(8,128)(2,1)} %copy-done, bf16[2,2,96,256]{3,2,1,0:T(8,128)(2,1)} %copy-done.1, ...), custom_call_target="tpu_custom_call" | custom-call | tf_op jit(solution)/shard_map/conv/pallas_call | solution.py:298
  60.8 0.0 all-to-all-done
  60.8 1.4 %reduce_sum.9 = f32[16,128]{1,0:T(8,128)S(1)} reduce(f32[128,16,128]{2,1,0:T(8,128)} %all-to-all-done, f32[]{:T(128)} %constant.0.clone.1), dimensions={0}, to_apply=%region_0.0 | reduce | flops 260096 | bytes 1056772 | tf_op jit(solution)/shard_map/reduce_sum | solution.py:514
  62.2 0.6 slice_multiply_fusion
Async XLA Ops:
  4.7 19.6 %collective-permute-start = (bf16[2,2,96,256]{3,2,1,0:T(8,128)(2,1)S(1)}, bf16[2,2,96,256]{3,2,1,0:T(8,128)(2,1)S(1)}, u32[]{:S(2)}, u32[]{:S(2)}) collective-permute-start(bf16[2,2,96,256]{3,2,1,0:T(8,128)(2,1)S(1)} %get-tuple-element.12.gxh_ref), channel_id=1, source_target_pairs={{0,16},{16,32},{32,48},{48,64},{64,80},{80,96},{96,112},{1,17},{17... | collective-permute-start | bytes 589832 | tf_op jit(solution)/shard_map/ppermute | solution.py:492
  9.2 15.1 %collective-permute-start.1 = (bf16[2,2,96,256]{3,2,1,0:T(8,128)(2,1)S(1)}, bf16[2,2,96,256]{3,2,1,0:T(8,128)(2,1)S(1)}, u32[]{:S(2)}, u32[]{:S(2)}) collective-permute-start(bf16[2,2,96,256]{3,2,1,0:T(8,128)(2,1)S(1)} %get-tuple-element.13.gxl_ref), channel_id=1, source_target_pairs={{16,0},{32,16},{48,32},{64,48},{80,64},{96,80},{112,96},{17,1},{33... | collective-permute-start | bytes 589832 | tf_op jit(solution)/shard_map/ppermute | solution.py:492
  11.1 13.2 %collective-permute-start.2 = (bf16[2,2,96,256]{3,2,1,0:T(8,128)(2,1)S(1)}, bf16[2,2,96,256]{3,2,1,0:T(8,128)(2,1)S(1)}, u32[]{:S(2)}, u32[]{:S(2)}) collective-permute-start(bf16[2,2,96,256]{3,2,1,0:T(8,128)(2,1)S(1)} %get-tuple-element.14.gyh_ref), channel_id=1, source_target_pairs={{0,1},{1,2},{2,3},{3,4},{4,5},{5,6},{6,7},{7,8},{8,9},{9,10},{10,1... | collective-permute-start | bytes 589832 | tf_op jit(solution)/shard_map/ppermute | solution.py:492
  14.7 9.7 %collective-permute-start.3 = (bf16[2,2,96,256]{3,2,1,0:T(8,128)(2,1)S(1)}, bf16[2,2,96,256]{3,2,1,0:T(8,128)(2,1)S(1)}, u32[]{:S(2)}, u32[]{:S(2)}) collective-permute-start(bf16[2,2,96,256]{3,2,1,0:T(8,128)(2,1)S(1)} %get-tuple-element.15.gyl_ref), channel_id=1, source_target_pairs={{1,0},{2,1},{3,2},{4,3},{5,4},{6,5},{7,6},{8,7},{9,8},{10,9},{11,1... | collective-permute-start | bytes 589832 | tf_op jit(solution)/shard_map/ppermute | solution.py:492
  24.3 3.5 %copy-start = (bf16[2,2,96,256]{3,2,1,0:T(8,128)(2,1)}, bf16[2,2,96,256]{3,2,1,0:T(8,128)(2,1)S(1)}, u32[]{:S(2)}) copy-start(bf16[2,2,96,256]{3,2,1,0:T(8,128)(2,1)S(1)} %collective-permute-done.xw_far.xw_ref) | copy-start | bytes 589828
  24.3 3.5 %copy-start.1 = (bf16[2,2,96,256]{3,2,1,0:T(8,128)(2,1)}, bf16[2,2,96,256]{3,2,1,0:T(8,128)(2,1)S(1)}, u32[]{:S(2)}) copy-start(bf16[2,2,96,256]{3,2,1,0:T(8,128)(2,1)S(1)} %collective-permute-done.1.xe_far.xe_ref) | copy-start | bytes 589828
  24.3 3.4 %copy-start.2 = (bf16[2,2,96,256]{3,2,1,0:T(8,128)(2,1)}, bf16[2,2,96,256]{3,2,1,0:T(8,128)(2,1)S(1)}, u32[]{:S(2)}) copy-start(bf16[2,2,96,256]{3,2,1,0:T(8,128)(2,1)S(1)} %collective-permute-done.2.ys_far.ys_ref) | copy-start | bytes 589828
  24.4 3.4 %copy-start.3 = (bf16[2,2,96,256]{3,2,1,0:T(8,128)(2,1)}, bf16[2,2,96,256]{3,2,1,0:T(8,128)(2,1)S(1)}, u32[]{:S(2)}) copy-start(bf16[2,2,96,256]{3,2,1,0:T(8,128)(2,1)S(1)} %collective-permute-done.3.yn_far.yn_ref) | copy-start | bytes 589828
  27.8 33.0 %all-to-all-start = ((f32[128,16,128]{2,1,0:T(8,128)}), f32[128,16,128]{2,1,0:T(8,128)}, u32[]{:S(2)}, u32[]{:S(2)}) async-start(f32[128,16,128]{2,1,0:T(8,128)} %bitcast.6), calls=%async_computation | async-start | bytes 2097152 | tf_op jit(solution)/shard_map/all_to_all | solution.py:512
